TPU v7x, 128 devices: a whole 4x4x4 slice. The times are simulated.
128 devices in a mesh: rows: 128 (over x, y, z, core).
Axes of the slice: x: 4, y: 4, z: 4, core: 2. Of those that a mesh axis runs over, the one named last changes fastest.
Arguments:
- points: float32 [49152, 256], P('rows'), may hold values from -6 to 6
- inv_scale: float32 [256], replicated, may hold values from 0.03 to 0.15
- noise: float32 [1], replicated, may hold values from 1 to 2
- prior: float32 [49152, 512], P('rows'), may hold values from -0.12 to 0.12
- active: int32 [3, 49152], P(None, 'rows'), may hold values from 0 to 1, as said below
- pivots: int32 [3, 128], replicated, may hold values from 0 to 49151, as said below
Outputs:
- new_factor: float32 [49152, 384], P('rows')
- residual_diag: float32 [49152], P('rows')
Inputs may be any that keep to these rules, and one draw needn't show every extreme that they name: Rows active in panel p + 1 are active in panel p. In panel 0 exactly 96 times the number of devices rows are active in all; no device holds more than 336 active rows in a panel, and some device holds exactly 336 in panel 0. All 384 pivots are distinct, and a pivot of panel p is active in panels 0 to p.
All inputs are finite; a program needn't handle non-finite values.
Results may differ from a plain program's by a relative error of at most 0.0003.
Values sent between devices are 32-bit elements; how exact they have to be, the bound alone decides.
No kernel may reach another device: no remote copies, remote signals or barrier semaphores. Data moves between devices by JAX's collectives and lax.ppermute only.
A program may use at most 64 MiB of HBM per device.

v0:
```python
import jax
import jax.numpy as jnp
from jax import lax
from jax.sharding import PartitionSpec as P

D = 256
PANEL = 128
PANELS = 3
HELP_ROWS = 96
BUSY = 336


def carried_in(part, axis, combine, identity):
    place = lax.axis_index(axis)
    gathered = lax.all_gather(part, axis)
    state = jnp.zeros_like(part) + jnp.asarray(identity, part.dtype)

    def one(hop, state):
        return combine(state, lax.dynamic_index_in_dim(gathered, hop, 0, False))

    return lax.fori_loop(0, place, one, state)


def kernel_rows(left_points, left_squares, right_points, right_squares):
    inner = jnp.dot(
        left_points,
        right_points.T,
        precision=lax.Precision.HIGHEST,
        preferred_element_type=jnp.float32,
    )
    return jnp.exp(-0.5 * (left_squares[:, None] + right_squares[None, :] - 2.0 * inner))


def correction_of(factor_rows, pivot_factor):
    return jnp.dot(
        factor_rows,
        pivot_factor.T,
        precision=lax.Precision.HIGHEST,
        preferred_element_type=jnp.float32,
    )


def solve_columns(
    points_rows,
    ids_rows,
    correction,
    pivot_points,
    pivot_squares,
    pivot_ids,
    lower_factor,
    noise_level,
):
    row_squares = jnp.sum(points_rows * points_rows, axis=1)
    residual = kernel_rows(points_rows, row_squares, pivot_points, pivot_squares)
    residual = residual + noise_level * (ids_rows[:, None] == pivot_ids[None, :]).astype(
        jnp.float32
    )
    residual = residual - correction
    return jax.scipy.linalg.solve_triangular(lower_factor, residual.T, lower=True).T


def compact_rows(values, helper_slot, width):
    empty = jnp.zeros((HELP_ROWS, width), values.dtype)
    return empty.at[helper_slot].set(values, mode="drop")


def local(points, inv_scale, noise, prior, active, pivots):
    rows_here = points.shape[0]
    devices = lax.axis_size("rows")
    device_index = lax.axis_index("rows")
    send_cap = (BUSY + devices - 1) // devices
    slots = devices * send_cap
    noise_level = noise[0]
    scaled = points * inv_scale[None, :]
    local_rows = jnp.arange(rows_here, dtype=jnp.int32)
    row_ids = device_index * rows_here + local_rows
    counts = jnp.sum(active, axis=1)
    offsets = carried_in(
        counts, "rows", lambda earlier, later: earlier + later, jnp.zeros_like(counts)
    )
    factor_now = prior
    columns = []
    for panel_index in range(PANELS):
        pivot_ids = pivots[panel_index]
        selector = (pivot_ids[:, None] == row_ids[None, :]).astype(jnp.float32)
        owned_points = jnp.dot(
            selector, scaled, precision=lax.Precision.HIGHEST, preferred_element_type=jnp.float32
        )
        owned_factor = jnp.dot(
            selector,
            factor_now,
            precision=lax.Precision.HIGHEST,
            preferred_element_type=jnp.float32,
        )
        pivot_points, pivot_factor = lax.psum((owned_points, owned_factor), "rows")
        pivot_squares = jnp.sum(pivot_points * pivot_points, axis=1)
        block_matrix = kernel_rows(pivot_points, pivot_squares, pivot_points, pivot_squares)
        block_matrix = block_matrix + noise_level * jnp.eye(PANEL, dtype=jnp.float32)
        block_matrix = block_matrix - correction_of(pivot_factor, pivot_factor)
        lower_factor = jnp.linalg.cholesky(block_matrix)
        is_active = active[panel_index]
        rank_here = jnp.cumsum(is_active) - is_active
        global_rank = offsets[panel_index] + rank_here
        target = jnp.where(
            is_active == 1, global_rank % devices * send_cap + rank_here // devices, slots
        )
        chosen = jnp.full((slots,), rows_here, jnp.int32).at[target].set(local_rows, mode="drop")
        slot_table = (
            jnp.full((slots,), HELP_ROWS, jnp.int32)
            .at[target]
            .set(global_rank // devices, mode="drop")
        )
        send_points = jnp.take(scaled, chosen, axis=0, mode="fill", fill_value=0.0).reshape(
            devices, send_cap, D
        )
        send_ids = (
            jnp.take(row_ids, chosen, axis=0, mode="fill", fill_value=-1)
            .astype(jnp.float32)
            .reshape(devices, send_cap)
        )
        send_slots = slot_table.astype(jnp.float32).reshape(devices, send_cap)
        chosen_factor = jnp.take(factor_now, chosen, axis=0, mode="fill", fill_value=0.0)
        send_factor = chosen_factor.reshape(devices, send_cap, chosen_factor.shape[1])
        got_points, got_factor, got_ids, got_slots = (
            lax.all_to_all(send_points, "rows", split_axis=0, concat_axis=0, tiled=True),
            lax.all_to_all(send_factor, "rows", split_axis=0, concat_axis=0, tiled=True),
            lax.all_to_all(send_ids, "rows", split_axis=0, concat_axis=0, tiled=True),
            lax.all_to_all(send_slots, "rows", split_axis=0, concat_axis=0, tiled=True),
        )
        helper_slot = got_slots.reshape(slots).astype(jnp.int32)
        compact_factor = compact_rows(
            got_factor.reshape(slots, got_factor.shape[2]), helper_slot, got_factor.shape[2]
        )
        correction = correction_of(compact_factor, pivot_factor)
        compact_points = compact_rows(got_points.reshape(slots, D), helper_slot, D)
        compact_ids = (
            jnp.full((HELP_ROWS,), -1, jnp.int32)
            .at[helper_slot]
            .set(got_ids.reshape(slots).astype(jnp.int32), mode="drop")
        )
        solved = solve_columns(
            compact_points,
            compact_ids,
            correction,
            pivot_points,
            pivot_squares,
            pivot_ids,
            lower_factor,
            noise_level,
        )
        send_back = jnp.take(solved, helper_slot, axis=0, mode="fill", fill_value=0.0).reshape(
            devices, send_cap, PANEL
        )
        returned = lax.all_to_all(send_back, "rows", split_axis=0, concat_axis=0, tiled=True)
        fresh = jnp.take(
            returned.reshape(slots, PANEL), target, axis=0, mode="fill", fill_value=0.0
        )
        columns.append(fresh)
        factor_now = jnp.concatenate([factor_now, fresh], axis=1)
    new_factor = jnp.concatenate(columns, axis=1)
    residual_diag = (
        1.0
        + noise_level
        - jnp.sum(prior * prior, axis=1)
        - jnp.sum(new_factor * new_factor, axis=1)
    )
    return (new_factor, residual_diag)


def solution(mesh):
    return jax.shard_map(
        local,
        mesh=mesh,
        in_specs=(P("rows", None), P(), P(), P("rows", None), P(None, "rows"), P()),
        out_specs=(P("rows", None), P("rows")),
        check_vma=False,
    )
```

profile of v0, /device:TPU:1, one launch (start us, length us, event | category | flops | bytes accessed | tf_op | source)
XLA Modules:
  0.0 769.6 jit_solution(5223825122197548950)
XLA Ops:
  9.2 68.6 %all-reduce = s32[384]{0:T(512)S(1)} all-reduce(s32[384]{0:T(512)S(1)} %dynamic-update-slice.2), channel_id=2, replica_groups=mesh['rows'=128] {'rows'}, use_global_device_ids=true, to_apply=%add | all-reduce | flops 384 | bytes 3072
  81.2 2.7 fusion.95
  83.9 2.9 scatter_custom_fusion
  87.6 9.1 %all-to-all-start = ((f32[128,1,3]{2,1,0:T(1,128)}), f32[128,1,3]{2,1,0:T(1,128)S(1)}, u32[]{:S(2)}, u32[]{:S(2)}) async-start(f32[128,1,3]{2,1,0:T(1,128)} %bitcast.4), calls=%async_computation | async-start | bytes 131072 | tf_op jit(solution)/shard_map/all_to_all | solution.py:128
  105.5 2.9 scatter_custom_fusion.11
  108.4 2.8 gather_fusion.12
  112.9 2.9 scatter_custom_fusion.6
  115.9 2.8 gather_fusion.8
  120.9 3.4 scatter_custom_fusion.1
  124.3 2.8 gather_fusion.4
  136.5 9.8 %all-to-all-start.2 = ((f32[128,1,3]{2,1,0:T(1,128)}), f32[128,1,3]{2,1,0:T(1,128)S(1)}, u32[]{:S(2)}, u32[]{:S(2)}) async-start(f32[128,1,3]{2,1,0:T(1,128)} %bitcast.10), calls=%async_computation.2 | async-start | bytes 131072 | tf_op jit(solution)/shard_map/all_to_all | solution.py:127
  147.4 3.1 scatter_custom_fusion.10
  150.5 3.1 scatter_custom_fusion.5
  159.8 9.8 %all-to-all-start.5 = ((f32[128,1,3]{2,1,0:T(1,128)}), f32[128,1,3]{2,1,0:T(1,128)S(1)}, u32[]{:S(2)}, u32[]{:S(2)}) async-start(f32[128,1,3]{2,1,0:T(1,128)} %bitcast.15), calls=%async_computation.5 | async-start | bytes 131072 | tf_op jit(solution)/shard_map/all_to_all | solution.py:128
  170.2 8.8 %all-to-all-done.5 = f32[128,1,3]{2,1,0:T(1,128)S(1)} async-done(((f32[128,1,3]{2,1,0:T(1,128)}), f32[128,1,3]{2,1,0:T(1,128)S(1)}, u32[]{:S(2)}, u32[]{:S(2)}) %all-to-all-start.5) | async-done | bytes 1568 | tf_op jit(solution)/shard_map/all_to_all | solution.py:128
  178.9 4.8 all-to-all-start.12
  184.7 8.4 %all-to-all-done.12 = f32[128,1,3]{2,1,0:T(1,128)S(1)} async-done(((f32[128,1,3]{2,1,0:T(1,128)}), f32[128,1,3]{2,1,0:T(1,128)S(1)}, u32[]{:S(2)}, u32[]{:S(2)}) %all-to-all-start.12) | async-done | bytes 1568 | tf_op jit(solution)/shard_map/all_to_all | solution.py:127
  193.1 4.7 all-to-all-start.7
  197.9 9.4 %all-to-all-done.7 = f32[128,1,3]{2,1,0:T(1,128)S(1)} async-done(((f32[128,1,3]{2,1,0:T(1,128)}), f32[128,1,3]{2,1,0:T(1,128)S(1)}, u32[]{:S(2)}, u32[]{:S(2)}) %all-to-all-start.7) | async-done | bytes 1568 | tf_op jit(solution)/shard_map/all_to_all | solution.py:127
  207.2 5.0 all-to-all-start.10
  213.3 8.3 %all-to-all-done.10 = f32[128,1,3]{2,1,0:T(1,128)S(1)} async-done(((f32[128,1,3]{2,1,0:T(1,128)}), f32[128,1,3]{2,1,0:T(1,128)S(1)}, u32[]{:S(2)}, u32[]{:S(2)}) %all-to-all-start.10) | async-done | bytes 1568 | tf_op jit(solution)/shard_map/all_to_all | solution.py:128
  221.6 4.8 all-to-all-start.1
  227.1 2.9 scatter_custom_fusion.3
  230.0 2.9 scatter_custom_fusion.8
  233.0 2.9 scatter_custom_fusion.13
  235.9 14.9 %all-reduce.12.cloned.1.call-done = (f32[128,512]{1,0:T(8,128)}, f32[128,256]{1,0:T(8,128)}) async-done(((f32[128,512]{1,0:T(8,128)}, f32[128,256]{1,0:T(8,128)}), (f32[128,512]{1,0:T(8,128)}, f32[128,256]{1,0:T(8,128)})) %all-reduce.12.cloned.1.call-update) | async-done | bytes 393232 | tf_op jit(solution)/shard_map/psum | solution.py:95
  254.6 7.5 all-to-all-start.3
  262.1 11.7 %cholesky.59 = f32[128,128]{1,0:T(8,128)S(1)} custom-call(f32[128,128]{1,0:T(8,128)S(1)} %fusion.65), custom_call_target="Cholesky" | custom-call | tf_op jit(solution)/shard_map/jit(cholesky)/cholesky | solution.py:100
  275.2 9.8 %custom-call.7 = f32[1,128,128]{1,2,0:T(8,128)S(1)} custom-call(f32[1,128,128]{2,1,0:T(8,128)S(1)} %fusion.57), custom_call_target="InvertDiagBlocksLowerTriangular" | custom-call | tf_op jit(solution)/shard_map/jit(_solve_triangular)/triangular_solve | solution.py:59
  287.2 9.8 %all-to-all-start.6 = ((f32[128,3,256]{2,1,0:T(4,128)}), f32[128,3,256]{2,1,0:T(4,128)S(1)}, u32[]{:S(2)}, u32[]{:S(2)}) async-start(f32[128,3,256]{2,1,0:T(4,128)} %reshape.700), calls=%async_computation.6 | async-start | bytes 1048576 | tf_op jit(solution)/shard_map/all_to_all | solution.py:125
  303.7 6.8 all-to-all-done.6
  310.5 4.7 all-to-all-start.4
  317.9 8.2 %all-to-all-done.4 = f32[128,3,128]{2,1,0:T(4,128)S(1)} async-done(((f32[128,3,128]{2,1,0:T(4,128)}), f32[128,3,128]{2,1,0:T(4,128)S(1)}, u32[]{:S(2)}, u32[]{:S(2)}) %all-to-all-start.4) | async-done | bytes 196640 | tf_op jit(solution)/shard_map/all_to_all | solution.py:154
  332.7 4.7 all-to-all-start.8
  337.4 146.0 %all-reduce.10.cloned.1.call-done = (f32[128,640]{1,0:T(8,128)}, f32[128,256]{1,0:T(8,128)}) async-done(((f32[128,640]{1,0:T(8,128)}, f32[128,256]{1,0:T(8,128)}), (f32[128,640]{1,0:T(8,128)}, f32[128,256]{1,0:T(8,128)})) %all-reduce.10.cloned.1.call-update) | async-done | bytes 458768 | tf_op jit(solution)/shard_map/psum | solution.py:95
  487.3 11.7 %cholesky.70 = f32[128,128]{1,0:T(8,128)S(1)} custom-call(f32[128,128]{1,0:T(8,128)S(1)} %fusion.63), custom_call_target="Cholesky" | custom-call | tf_op jit(solution)/shard_map/jit(cholesky)/cholesky | solution.py:100
  500.4 9.8 %custom-call.8 = f32[1,128,128]{1,2,0:T(8,128)S(1)} custom-call(f32[1,128,128]{2,1,0:T(8,128)S(1)} %fusion.58), custom_call_target="InvertDiagBlocksLowerTriangular" | custom-call | tf_op jit(solution)/shard_map/jit(_solve_triangular)/triangular_solve | solution.py:59
  510.2 5.8 all-to-all-start.11
  523.0 6.5 all-to-all-done.11
  529.5 4.7 all-to-all-start.9
  536.5 8.7 %all-to-all-done.9 = f32[128,3,128]{2,1,0:T(4,128)S(1)} async-done(((f32[128,3,128]{2,1,0:T(4,128)}), f32[128,3,128]{2,1,0:T(4,128)S(1)}, u32[]{:S(2)}, u32[]{:S(2)}) %all-to-all-start.9) | async-done | bytes 196640 | tf_op jit(solution)/shard_map/all_to_all | solution.py:154
  553.6 5.0 all-to-all-start.13
  558.7 149.4 %all-reduce.8.cloned.1.call-done = (f32[128,256]{1,0:T(8,128)}, f32[128,768]{1,0:T(8,128)}) async-done(((f32[128,256]{1,0:T(8,128)}, f32[128,768]{1,0:T(8,128)}), (f32[128,256]{1,0:T(8,128)}, f32[128,768]{1,0:T(8,128)})) %all-reduce.8.cloned.1.call-update) | async-done | bytes 524304 | tf_op jit(solution)/shard_map/psum | solution.py:95
  712.1 11.7 %cholesky.81 = f32[128,128]{1,0:T(8,128)S(1)} custom-call(f32[128,128]{1,0:T(8,128)S(1)} %fusion.61), custom_call_target="Cholesky" | custom-call | tf_op jit(solution)/shard_map/jit(cholesky)/cholesky | solution.py:100
  725.2 9.8 %custom-call.9 = f32[1,128,128]{1,2,0:T(8,128)S(1)} custom-call(f32[1,128,128]{2,1,0:T(8,128)S(1)} %fusion.59), custom_call_target="InvertDiagBlocksLowerTriangular" | custom-call | tf_op jit(solution)/shard_map/jit(_solve_triangular)/triangular_solve | solution.py:59
  736.8 2.6 scatter_custom_fusion.14
  742.2 7.0 all-to-all-start.14
  749.3 10.6 %all-to-all-done.14 = f32[128,3,128]{2,1,0:T(4,128)S(1)} async-done(((f32[128,3,128]{2,1,0:T(4,128)}), f32[128,3,128]{2,1,0:T(4,128)S(1)}, u32[]{:S(2)}, u32[]{:S(2)}) %all-to-all-start.14) | async-done | bytes 196640 | tf_op jit(solution)/shard_map/all_to_all | solution.py:154
  (213 shorter events, 96.7 us)
Async XLA Ops:
  7.2 91.5 %copy-start = (f32[384,512]{1,0:T(8,128)S(1)}, f32[384,512]{1,0:T(8,128)}, u32[]{:S(2)}) copy-start(f32[384,512]{1,0:T(8,128)} %param.22) | copy-start | bytes 2359300
  83.9 21.6 %copy-start.9 = (s32[384]{0:T(512)}, s32[384]{0:T(512)S(1)}, u32[]{:S(2)}) copy-start(s32[384]{0:T(512)S(1)} %get-tuple-element.34) | copy-start | bytes 4612
  83.9 29.0 %copy-start.8 = (s32[384]{0:T(512)}, s32[384]{0:T(512)S(1)}, u32[]{:S(2)}) copy-start(s32[384]{0:T(512)S(1)} %get-tuple-element.32) | copy-start | bytes 4612
  87.6 48.8 %all-to-all-start = ((f32[128,1,3]{2,1,0:T(1,128)}), f32[128,1,3]{2,1,0:T(1,128)S(1)}, u32[]{:S(2)}, u32[]{:S(2)}) async-start(f32[128,1,3]{2,1,0:T(1,128)} %bitcast.4), calls=%async_computation | async-start | bytes 131072 | tf_op jit(solution)/shard_map/all_to_all | solution.py:128
  96.8 154.0 %all-reduce.12.cloned.1.call-start = ((), (), s32[]{:S(2)}) async-start(), calls=%async_computation.17 | async-start | bytes 786432 | tf_op jit(solution)/shard_map/psum | solution.py:95
  136.5 23.3 %all-to-all-start.2 = ((f32[128,1,3]{2,1,0:T(1,128)}), f32[128,1,3]{2,1,0:T(1,128)S(1)}, u32[]{:S(2)}, u32[]{:S(2)}) async-start(f32[128,1,3]{2,1,0:T(1,128)} %bitcast.10), calls=%async_computation.2 | async-start | bytes 131072 | tf_op jit(solution)/shard_map/all_to_all | solution.py:127
  159.8 19.2 %all-to-all-start.5 = ((f32[128,1,3]{2,1,0:T(1,128)}), f32[128,1,3]{2,1,0:T(1,128)S(1)}, u32[]{:S(2)}, u32[]{:S(2)}) async-start(f32[128,1,3]{2,1,0:T(1,128)} %bitcast.15), calls=%async_computation.5 | async-start | bytes 131072 | tf_op jit(solution)/shard_map/all_to_all | solution.py:128
  178.9 14.2 %all-to-all-start.12 = ((f32[128,1,3]{2,1,0:T(1,128)}), f32[128,1,3]{2,1,0:T(1,128)S(1)}, u32[]{:S(2)}, u32[]{:S(2)}) async-start(f32[128,1,3]{2,1,0:T(1,128)} %bitcast.30), calls=%async_computation.12 | async-start | bytes 131072 | tf_op jit(solution)/shard_map/all_to_all | solution.py:127
  193.1 14.1 %all-to-all-start.7 = ((f32[128,1,3]{2,1,0:T(1,128)}), f32[128,1,3]{2,1,0:T(1,128)S(1)}, u32[]{:S(2)}, u32[]{:S(2)}) async-start(f32[128,1,3]{2,1,0:T(1,128)} %bitcast.20), calls=%async_computation.7 | async-start | bytes 131072 | tf_op jit(solution)/shard_map/all_to_all | solution.py:127
  207.2 14.4 %all-to-all-start.10 = ((f32[128,1,3]{2,1,0:T(1,128)}), f32[128,1,3]{2,1,0:T(1,128)S(1)}, u32[]{:S(2)}, u32[]{:S(2)}) async-start(f32[128,1,3]{2,1,0:T(1,128)} %bitcast.25), calls=%async_computation.10 | async-start | bytes 131072 | tf_op jit(solution)/shard_map/all_to_all | solution.py:128
  221.6 32.9 %all-to-all-start.1 = ((f32[128,3,256]{2,1,0:T(4,128)}), f32[128,3,256]{2,1,0:T(4,128)S(1)}, u32[]{:S(2)}, u32[]{:S(2)}) async-start(f32[128,3,256]{2,1,0:T(4,128)} %reshape.693), calls=%async_computation.1 | async-start | bytes 1048576 | tf_op jit(solution)/shard_map/all_to_all | solution.py:125
  254.6 32.6 %all-to-all-start.3 = ((f32[128,3,512]{2,1,0:T(4,128)}), f32[128,3,512]{2,1,0:T(4,128)S(1)}, u32[]{:S(2)}, u32[]{:S(2)}) async-start(f32[128,3,512]{2,1,0:T(4,128)} %broadcast_select_fusion.2), calls=%async_computation.3 | async-start | bytes 2097152 | tf_op jit(solution)/shard_map/all_to_all | solution.py:126
  287.2 23.3 %all-to-all-start.6 = ((f32[128,3,256]{2,1,0:T(4,128)}), f32[128,3,256]{2,1,0:T(4,128)S(1)}, u32[]{:S(2)}, u32[]{:S(2)}) async-start(f32[128,3,256]{2,1,0:T(4,128)} %reshape.700), calls=%async_computation.6 | async-start | bytes 1048576 | tf_op jit(solution)/shard_map/all_to_all | solution.py:125
  297.0 3.8 copy-start.3
  297.0 4.2 copy-start.4
  310.5 15.6 %all-to-all-start.4 = ((f32[128,3,128]{2,1,0:T(4,128)}), f32[128,3,128]{2,1,0:T(4,128)S(1)}, u32[]{:S(2)}, u32[]{:S(2)}) async-start(f32[128,3,128]{2,1,0:T(4,128)} %reshape.696), calls=%async_computation.4 | async-start | bytes 524288 | tf_op jit(solution)/shard_map/all_to_all | solution.py:154
  315.2 168.1 %all-reduce.10.cloned.1.call-start = ((), (), s32[]{:S(2)}) async-start(), calls=%async_computation.16 | async-start | bytes 917504 | tf_op jit(solution)/shard_map/psum | solution.py:95
  317.8 9.6 %copy-start.7 = (pred[384]{0:T(512)(128)(4,1)S(1)}, pred[384]{0:T(512)(128)(4,1)}, u32[]{:S(2)}) copy-start(pred[384]{0:T(512)(128)(4,1)} %get-tuple-element.62) | copy-start | bytes 1156
  332.7 177.5 %all-to-all-start.8 = ((f32[128,3,640]{2,1,0:T(4,128)}), f32[128,3,640]{2,1,0:T(4,128)S(1)}, u32[]{:S(2)}, u32[]{:S(2)}) async-start(f32[128,3,640]{2,1,0:T(4,128)} %broadcast_select_fusion.1), calls=%async_computation.8 | async-start | bytes 2621440 | tf_op jit(solution)/shard_map/all_to_all | solution.py:126
  510.2 19.3 %all-to-all-start.11 = ((f32[128,3,256]{2,1,0:T(4,128)}), f32[128,3,256]{2,1,0:T(4,128)S(1)}, u32[]{:S(2)}, u32[]{:S(2)}) async-start(f32[128,3,256]{2,1,0:T(4,128)} %reshape.707), calls=%async_computation.11 | async-start | bytes 1048576 | tf_op jit(solution)/shard_map/all_to_all | solution.py:125
  516.0 4.0 copy-start.2
  516.0 4.5 copy-start.5
  529.5 15.6 %all-to-all-start.9 = ((f32[128,3,128]{2,1,0:T(4,128)}), f32[128,3,128]{2,1,0:T(4,128)S(1)}, u32[]{:S(2)}, u32[]{:S(2)}) async-start(f32[128,3,128]{2,1,0:T(4,128)} %reshape.703), calls=%async_computation.9 | async-start | bytes 524288 | tf_op jit(solution)/shard_map/all_to_all | solution.py:154
  534.2 173.8 %all-reduce.8.cloned.1.call-start = ((), (), s32[]{:S(2)}) async-start(), calls=%async_computation.15 | async-start | bytes 1048576 | tf_op jit(solution)/shard_map/psum | solution.py:95
  553.6 181.7 %all-to-all-start.13 = ((f32[128,3,768]{2,1,0:T(4,128)}), f32[128,3,768]{2,1,0:T(4,128)S(1)}, u32[]{:S(2)}, u32[]{:S(2)}) async-start(f32[128,3,768]{2,1,0:T(4,128)} %broadcast_select_fusion), calls=%async_computation.13 | async-start | bytes 3145728 | tf_op jit(solution)/shard_map/all_to_all | solution.py:126
  708.0 27.0 %copy-start.6 = (f32[128,256]{1,0:T(8,128)S(1)}, f32[128,256]{1,0:T(8,128)}, u32[]{:S(2)}) copy-start(f32[128,256]{1,0:T(8,128)} %get-tuple-element.46) | copy-start | bytes 393220
  735.3 4.1 copy-start.1
  742.2 17.8 %all-to-all-start.14 = ((f32[128,3,128]{2,1,0:T(4,128)}), f32[128,3,128]{2,1,0:T(4,128)S(1)}, u32[]{:S(2)}, u32[]{:S(2)}) async-start(f32[128,3,128]{2,1,0:T(4,128)} %reshape.710), calls=%async_computation.14 | async-start | bytes 524288 | tf_op jit(solution)/shard_map/all_to_all | solution.py:154
Sparse Core Ops, SparseCore 0:
  102.4 148.3 all-reduce.11
  331.3 151.9 all-reduce.9
  552.2 155.8 all-reduce.7
where the time goes:
time: 779 us; the launch traced here: 770 us
  waiting for transfers between devices  386 us (50%)
  starting transfers between devices  97.8 us (13%)
  other arithmetic  92.7 us (12%)
  local copies, waits for them, and re-layouts  90.6 us (12%)
  blocking collectives  68.6 us (9%)
  matrix products  18 us (2%)
  between operations  15.8 us (2%)
    psum x3, waiting for transfers between devices, local(): pivot_points, pivot_factor = lax.psum((owned_points, owned_factor), 'rows')  310 us
    unnamed x1, blocking collectives  68.6 us
    another operation x9, other arithmetic, local(): lower_factor = jnp.linalg.cholesky(block_matrix)  37.2 us
    another operation x6, other arithmetic, solve_columns(): jax.scipy.linalg.solve_triangular(lower_factor, residual.T, lower=True)  31.4 us
    all_to_all x3, waiting for transfers between devices, local(): lax.all_to_all(send_back, 'rows', split_axis=0, concat_axis=0, tiled=True)  27.5 us
    all_to_all x3, starting transfers between devices, local(): lax.all_to_all(send_slots, 'rows', split_axis=0, concat_axis=0, tiled=True)  23.9 us
    all_to_all x3, starting transfers between devices, local(): lax.all_to_all(send_points, 'rows', split_axis=0, concat_axis=0, tiled=True)  20.3 us
    all_to_all x3, starting transfers between devices, local(): lax.all_to_all(send_ids, 'rows', split_axis=0, concat_axis=0, tiled=True)  19.3 us
  transfers between devices with their start and end apart: 18, of which 12 were waited for; matrix products, arithmetic and copies ran while one was open for 21% of the time, Pallas kernels for 0%

commit v1 on v0

v1 whole, which is shorter than its diff:
```python
import functools

import jax
import jax.numpy as jnp
from jax import lax
from jax.experimental import pallas as pl
from jax.experimental.pallas import tpu as pltpu
from jax.sharding import PartitionSpec as P

D = 256
R0 = 512
F = D + R0
PANEL = 128
PANELS = 3
PIV = PANEL * PANELS
HALF = PIV // 2
STRIP = 16
HI = lax.Precision.HIGHEST
BF = jnp.bfloat16
F32 = jnp.float32
NT = (((1,), (1,)), ((), ()))
NN = (((1,), (0,)), ((), ()))


def dot_hi(a, b, dims=NT):
    return lax.dot_general(a, b, dims, precision=HI, preferred_element_type=F32)


def split2(a):
    high = a.astype(BF)
    return high, (a - high.astype(F32)).astype(BF)


def split3(a):
    high, rest = a.astype(BF), None
    rest = a - high.astype(F32)
    mid = rest.astype(BF)
    return high, mid, (rest - mid.astype(F32)).astype(BF)


def dot_bf(a, b, dims=NT):
    return lax.dot_general(a, b, dims, preferred_element_type=F32)


def dot_x3(a, b, dims=NT):
    ah, al = split2(a)
    bh, bl = split2(b)
    return dot_bf(ah, bh, dims) + (dot_bf(ah, bl, dims) + dot_bf(al, bh, dims))


def column_of(row):
    return jnp.transpose(jnp.broadcast_to(row, (8, 128)))[:, 0:1]


def pack_kernel(place_ref, pivots_ref, points_ref, prior_ref, keep_ref, give_ref, all_ref):
    rows = points_ref.shape[0]
    core = place_ref[0]
    base = (place_ref[1] * rows).astype(F32)
    lanes = lax.broadcasted_iota(jnp.int32, (PANEL, rows), 1).astype(F32)
    parts = [split3(points_ref[...]), split3(prior_ref[...])]
    for panel in range(PANELS):
        wanted = column_of(pivots_ref[panel : panel + 1, :].astype(F32)) - base
        select = (lanes == wanted).astype(BF)
        at = 0
        for high, mid, low in parts:
            got = dot_bf(select, high, NN) + dot_bf(select, mid, NN)
            got = got + dot_bf(select, low, NN)
            all_ref[panel * PANEL : (panel + 1) * PANEL, at : at + got.shape[1]] = got
            at += got.shape[1]
    keep_ref[...] = all_ref[pl.ds(pl.multiple_of(core * HALF, HALF), HALF), :]
    give_ref[...] = all_ref[pl.ds(pl.multiple_of((1 - core) * HALF, HALF), HALF), :]


def fold_kernel(keep_ref, came_ref, out_ref):
    homes = out_ref.shape[0]
    for turn in range(HALF // homes):
        span = pl.ds(turn * homes, homes)
        out_ref[:, 0, turn * F : (turn + 1) * F] = keep_ref[span, :] + came_ref[span, :]


def factor(w_ref, z_ref, inv_ref):
    size = PANEL
    iota = lax.broadcasted_iota(jnp.int32, (STRIP, size), 0)
    wide = (STRIP, size)
    z_ref[...] = jnp.zeros_like(z_ref)
    for first in range(0, size, STRIP):
        left = w_ref[first : first + STRIP, 0:size]
        right = w_ref[first : first + STRIP, size : 2 * size]
        columns = [
            jnp.broadcast_to(left[:, first + j : first + j + 1], wide) for j in range(STRIP)
        ]
        for j in range(STRIP):
            root = lax.rsqrt(jnp.broadcast_to(columns[j][j : j + 1, :], wide))
            inverse = root * root
            row_left = jnp.broadcast_to(left[j : j + 1, :], wide)
            row_right = jnp.broadcast_to(right[j : j + 1, :], wide)
            inv_ref[first + j : first + j + 1, :] = row_right[0:1] * root[0:1]
            weight = jnp.where(iota == j, 1.0 - inverse, columns[j] * inverse)
            left = left - weight * row_left
            right = right - weight * row_right
            for m in range(j + 1, STRIP):
                columns[m] = columns[m] - weight * jnp.broadcast_to(columns[m][j : j + 1, :], wide)
        last = first + STRIP
        if last < size:
            z_ref[first:last, 0:size] = left
            z_ref[first:last, size : 2 * size] = right
            below = w_ref[last:size, 0:size]
            w_ref[last:size, :] = w_ref[last:size, :] - dot_hi(below, z_ref[...], NN)
            z_ref[first:last, :] = jnp.zeros((STRIP, 2 * size), F32)


def window_kernel(
    place_ref,
    noise_ref,
    pivots_ref,
    scale_ref,
    points_ref,
    prior_ref,
    active_ref,
    mine_ref,
    other_ref,
    new_ref,
    diag_ref,
    pp_ref,
    pf_ref,
    k_ref,
    w_ref,
    z_ref,
    inv_ref,
    x_ref,
):
    rows = points_ref.shape[0]
    homes = mine_ref.shape[0]
    core = place_ref[0]
    base = place_ref[1] * rows
    noise = noise_ref[0]
    scale = scale_ref[...]
    for turn in range(HALF // homes):
        for ref, half in ((mine_ref, core), (other_ref, 1 - core)):
            at = pl.ds(pl.multiple_of(half * HALF, HALF) + turn * homes, homes)
            pp_ref[at, :] = ref[:, 0, turn * F : turn * F + D] * scale
            pf_ref[at, :] = ref[:, 0, turn * F + D : (turn + 1) * F]
    ones = jnp.ones((8, D), F32)
    pp = pp_ref[...]
    pf = pf_ref[...]
    pp2 = pp * pp
    square_row = dot_hi(ones, pp2)[0:1, :]
    square_col = jnp.sum(pp2, axis=1, keepdims=True)
    mine = points_ref[...] * scale
    prior = prior_ref[...]
    mine_col = jnp.sum(mine * mine, axis=1, keepdims=True)
    eye = (
        lax.broadcasted_iota(jnp.int32, (PIV, PIV), 0)
        == lax.broadcasted_iota(jnp.int32, (PIV, PIV), 1)
    ).astype(F32)
    gram = jnp.exp(-0.5 * (square_col + square_row - 2.0 * dot_hi(pp, pp))) + noise * eye
    k_ref[...] = gram - dot_hi(pf, pf)
    residual = jnp.exp(-0.5 * (mine_col + square_row - 2.0 * dot_hi(mine, pp)))
    residual = residual - dot_hi(prior, pf)
    ids = base + lax.broadcasted_iota(jnp.int32, (rows, PANEL), 0)
    for panel in range(PANELS):
        span = slice(panel * PANEL, (panel + 1) * PANEL)
        same = (ids == pivots_ref[panel : panel + 1, :]).astype(F32)
        x_ref[:, span] = residual[:, span] + noise * same
    small_eye = eye[0:PANEL, 0:PANEL]
    total = dot_hi(jnp.ones((8, R0), F32), prior * prior)[0:1, :]
    for panel in range(PANELS):
        span = slice(panel * PANEL, (panel + 1) * PANEL)
        w_ref[:, 0:PANEL] = k_ref[span, span]
        w_ref[:, PANEL:] = small_eye
        factor(w_ref, z_ref, inv_ref)
        inverse = inv_ref[...]
        x_ref[:, span] = dot_hi(x_ref[:, span], inverse)
        if panel + 1 < PANELS:
            rest = slice((panel + 1) * PANEL, PIV)
            below = dot_hi(k_ref[rest, span], inverse)
            k_ref[rest, rest] = k_ref[rest, rest] - dot_hi(below, below)
            x_ref[:, rest] = x_ref[:, rest] - dot_hi(x_ref[:, span], below)
    for panel in range(PANELS):
        span = slice(panel * PANEL, (panel + 1) * PANEL)
        for block in range(rows // 128):
            here = slice(block * 128, (block + 1) * 128)
            mask = column_of(active_ref[panel : panel + 1, here].astype(F32))
            new_ref[here, span] = x_ref[here, span] * mask
    new = new_ref[...]
    total = total + dot_hi(jnp.ones((8, PIV), F32), new * new)[0:1, :]
    diag_ref[...] = 1.0 + noise - total


SMEM = pl.BlockSpec(memory_space=pltpu.SMEM)
VMEM = pl.BlockSpec(memory_space=pltpu.VMEM)


def local(points, inv_scale, noise, prior, active, pivots):
    rows = points.shape[0]
    devices = lax.axis_size("rows")
    homes = devices // 2
    index = lax.axis_index("rows")
    place = jnp.stack([index % 2, index]).astype(jnp.int32)
    partner = [(i, i ^ 1) for i in range(devices)]
    groups = [[2 * chip + core for chip in range(homes)] for core in range(2)]
    half = jax.ShapeDtypeStruct((HALF, F), F32)
    keep, give = pl.pallas_call(
        pack_kernel,
        out_shape=(half, half),
        in_specs=[SMEM, VMEM, VMEM, VMEM],
        out_specs=(VMEM, VMEM),
        scratch_shapes=[pltpu.VMEM((PIV, F), F32)],
        name="pack",
    )(place, pivots, points, prior)
    came = lax.ppermute(give, "rows", partner)
    wide = jax.ShapeDtypeStruct((homes, 1, HALF // homes * F), F32)
    spread = pl.pallas_call(
        fold_kernel, out_shape=wide, in_specs=[VMEM, VMEM], out_specs=VMEM, name="fold"
    )(keep, came)
    exchange = functools.partial(
        lax.all_to_all,
        axis_name="rows",
        split_axis=0,
        concat_axis=0,
        axis_index_groups=groups,
        tiled=True,
    )
    got = exchange(spread)
    owned = jnp.broadcast_to(jnp.sum(got, axis=0, keepdims=True), wide.shape)
    mine = exchange(owned)
    other = lax.ppermute(mine, "rows", partner)
    new, diag = pl.pallas_call(
        window_kernel,
        out_shape=(
            jax.ShapeDtypeStruct((rows, PIV), F32),
            jax.ShapeDtypeStruct((1, rows), F32),
        ),
        in_specs=[SMEM, SMEM] + [VMEM] * 7,
        out_specs=(VMEM, VMEM),
        scratch_shapes=[
            pltpu.VMEM((PIV, D), F32),
            pltpu.VMEM((PIV, R0), F32),
            pltpu.VMEM((PIV, PIV), F32),
            pltpu.VMEM((PANEL, 2 * PANEL), F32),
            pltpu.VMEM((PANEL, 2 * PANEL), F32),
            pltpu.VMEM((PANEL, PANEL), F32),
            pltpu.VMEM((rows, PIV), F32),
        ],
        name="window",
    )(place, noise, pivots, inv_scale.reshape(1, D), points, prior, active, mine, other)
    return (new, diag.reshape(rows))


def solution(mesh):
    return jax.shard_map(
        local,
        mesh=mesh,
        in_specs=(P("rows", None), P(), P(), P("rows", None), P(None, "rows"), P()),
        out_specs=(P("rows", None), P("rows")),
        check_vma=False,
    )
```

time: 779 us -> 79.9 us (0.10); the launches traced: 770 us -> 79.6 us
  waiting for transfers between devices: 386 us -> 2.82 us
  starting transfers between devices: 97.8 us -> 4.81 us
  other arithmetic: 92.7 us -> 1.56 us
  local copies, waits for them, and re-layouts: 90.6 us -> 2.6 us
  blocking collectives: 68.6 us -> 39.9 us
  Pallas kernels: 0 us -> 26.6 us
  matrix products: 18 us -> 0 us
  between operations: 15.8 us -> 1.3 us
    psum x3 -> x0, waiting for transfers between devices: 310 us -> none  [local(): pivot_points, pivot_factor = lax.psum((owned_points, owned_factor), 'rows')]
    all_to_all x15 -> x0, starting transfers between devices: 97.2 us -> none  [the longest x3 23.9 us: local(): lax.all_to_all(send_slots, 'rows', split_axis=0, concat_axis=0, tiled=True)]
    all_to_all x15 -> x0, waiting for transfers between devices: 75.7 us -> none  [the longest x3 27.5 us: local(): lax.all_to_all(send_back, 'rows', split_axis=0, concat_axis=0, tiled=True)]
    another operation x21 -> x1, other arithmetic: 69.6 us -> 0.61 us  [local(): place = jnp.stack([index % 2, index]).astype(jnp.int32)]
    unnamed x1 -> x0, blocking collectives: 68.6 us -> none
    scatter x15 -> x0, local copies, waits for them, and re-layouts: 40.2 us -> none  [the longest x6 13.2 us: compact_rows(): return empty.at[helper_slot].set(values, mode='drop')]
    all_to_all x0 -> x2, blocking collectives: none -> 39.9 us  [the longest x1 23.9 us: local(): got = exchange(spread)]
    gather x18 -> x0, local copies, waits for them, and re-layouts: 29 us -> none  [the longest x3 8.43 us: local(): jnp.take(row_ids, chosen, axis=0, mode='fill', fill_value=-1)]
  transfers between devices with their start and end apart: 18 -> 2, of which waited for: 12 -> 2; matrix products, arithmetic and copies ran while one was open for 21% -> 0% of each run, Pallas kernels for 0% -> 0%
where the time goes in v1:
time: 79.9 us; the launch traced here: 79.6 us
  blocking collectives  39.9 us (50%)
  Pallas kernels  26.6 us (33%)
  starting transfers between devices  4.81 us (6%)
  waiting for transfers between devices  2.82 us (4%)
  local copies, waits for them, and re-layouts  2.6 us (3%)
  other arithmetic  1.56 us (2%)
  between operations  1.3 us (2%)
    all_to_all x1, blocking collectives, local(): got = exchange(spread)  23.9 us
    pallas_call x1, Pallas kernels, local(): pl.pallas_call(window_kernel, out_shape=(jax.ShapeDtypeStruct((rows, PIV)...  20.8 us
    all_to_all x1, blocking collectives, local(): mine = exchange(owned)  16 us
    pallas_call x1, Pallas kernels, local(): pl.pallas_call(pack_kernel, out_shape=(half, half), in_specs=[SMEM, VMEM,...  3.55 us
    ppermute x1, starting transfers between devices, local(): other = lax.ppermute(mine, 'rows', partner)  3.43 us
    unnamed x8, local copies, waits for them, and re-layouts  2.29 us
    pallas_call x1, Pallas kernels, local(): pl.pallas_call(fold_kernel, out_shape=wide, in_specs=[VMEM, VMEM], out_sp...  2.19 us
    ppermute x1, waiting for transfers between devices, local(): came = lax.ppermute(give, 'rows', partner)  1.84 us
  transfers between devices with their start and end apart: 2, of which 2 were waited for; matrix products, arithmetic and copies ran while one was open for 0% of the time, Pallas kernels for 0%

profile of v1, /device:TPU:1, one launch (start us, length us, event | category | flops | bytes accessed | tf_op | source)
XLA Modules:
  0.0 79.6 jit_solution(12586870484253767611)
XLA Ops:
  0.6 0.6 pad_add_fusion.place_ref
  1.2 3.6 %pack.1 = (f32[192,768]{1,0:T(8,128)}, f32[192,768]{1,0:T(8,128)}) custom-call(s32[2]{0:T(128)} %pad_add_fusion.place_ref, s32[3,128]{1,0:T(4,128)} %pivots_ref.3, f32[384,256]{1,0:T(8,128)} %points_ref.3, f32[384,512]{1,0:T(8,128)} %prior_ref.3), custom_call_target="tpu_custom_call" | custom-call | tf_op jit(solution)/shard_map/pack/pallas_call | solution.py:203
  4.8 1.4 %collective-permute-start = (f32[192,768]{1,0:T(8,128)}, f32[192,768]{1,0:T(8,128)S(1)}, u32[]{:S(2)}, u32[]{:S(2)}) collective-permute-start(f32[192,768]{1,0:T(8,128)} %get-tuple-element.7), channel_id=1, source_target_pairs={{0,1},{1,0},{2,3},{3,2},{4,5},{5,4},{6,7},{7,6},{8,9},{9,8},{10,11... | collective-permute-start | bytes 1769480 | tf_op jit(solution)/shard_map/ppermute | solution.py:211
  6.2 1.8 %collective-permute-done.came_ref = f32[192,768]{1,0:T(8,128)S(1)} collective-permute-done((f32[192,768]{1,0:T(8,128)}, f32[192,768]{1,0:T(8,128)S(1)}, u32[]{:S(2)}, u32[]{:S(2)}) %collective-permute-start) | collective-permute-done | bytes 589856 | tf_op jit(solution)/shard_map/ppermute | solution.py:211
  8.0 0.0 copy-start.1
  8.0 0.8 %copy-done.1 = f32[192,768]{1,0:T(8,128)} copy-done((f32[192,768]{1,0:T(8,128)}, f32[192,768]{1,0:T(8,128)S(1)}, u32[]{:S(2)}) %copy-start.1) | copy-done | bytes 589848
  8.8 2.2 %fold.1 = f32[64,1,2304]{2,1,0:T(1,128)} custom-call(f32[192,768]{1,0:T(8,128)} %get-tuple-element.6.keep_ref, f32[192,768]{1,0:T(8,128)} %copy-done.1), custom_call_target="tpu_custom_call" | custom-call | tf_op jit(solution)/shard_map/fold/pallas_call | solution.py:213
  11.0 23.9 %all_to_all.10 = f32[64,1,2304]{2,1,0:T(1,128)S(1)} all-to-all(f32[64,1,2304]{2,1,0:T(1,128)} %fold.1), channel_id=1, replica_groups={{0,2,4,6,8,10,12,14,16,18,20,22,24,26,28,30,32,34,36,38,40,42,44,46,48,..., dimensions={0} | all-to-all | bytes 1179648 | tf_op jit(solution)/shard_map/all_to_all | solution.py:224
  34.9 0.4 reduce_sum.9
  35.2 0.3 broadcast_in_dim.2
  35.6 16.0 %all_to_all.11.mine_ref = f32[64,1,2304]{2,1,0:T(1,128)S(1)} all-to-all(f32[64,1,2304]{2,1,0:T(1,128)S(1)} %broadcast_in_dim.2), channel_id=1, replica_groups={{0,2,4,6,8,10,12,14,16,18,20,22,24,26,28,30,32,34,36,38,40,42,44,46,48,..., dimensions={0} | all-to-all | bytes 1179648 | tf_op jit(solution)/shard_map/all_to_all | solution.py:226
  51.6 0.0 copy-start
  51.6 3.4 %collective-permute-start.1 = (f32[64,1,2304]{2,1,0:T(1,128)S(1)}, f32[64,1,2304]{2,1,0:T(1,128)S(1)}, u32[]{:S(2)}, u32[]{:S(2)}) collective-permute-start(f32[64,1,2304]{2,1,0:T(1,128)S(1)} %all_to_all.11.mine_ref), channel_id=1, source_target_pairs={{0,1},{1,0},{2,3},{3,2},{4,5},{5,4},{6,7},{7,6},{8,9},{9,8},{10,11... | collective-permute-start | bytes 1769480 | tf_op jit(solution)/shard_map/ppermute | solution.py:227
  55.7 1.0 %collective-permute-done.1.other_ref = f32[64,1,2304]{2,1,0:T(1,128)S(1)} collective-permute-done((f32[64,1,2304]{2,1,0:T(1,128)S(1)}, f32[64,1,2304]{2,1,0:T(1,128)S(1)}, u32[]{:S(2)}, u32[]{:S(2)}) %collective-permute-start.1) | collective-permute-done | bytes 589856 | tf_op jit(solution)/shard_map/ppermute | solution.py:227
  56.7 0.0 copy-start.2
  56.7 0.0 copy-done
  56.7 0.8 %copy-done.2 = f32[64,1,2304]{2,1,0:T(1,128)} copy-done((f32[64,1,2304]{2,1,0:T(1,128)}, f32[64,1,2304]{2,1,0:T(1,128)S(1)}, u32[]{:S(2)}) %copy-start.2) | copy-done | bytes 589848
  57.5 20.8 %window.1 = (f32[384,384]{1,0:T(8,128)}, f32[1,384]{1,0:T(1,128)}) custom-call(s32[2]{0:T(128)} %pad_add_fusion.place_ref, f32[1]{0:T(128)S(6)} %copy.8.noise_ref, s32[3,128]{1,0:T(4,128)} %pivots_ref.3, f32[1,256]{1,0:T(1,128)} %bitcast.3, f32[384,256]{1,0:T(8,128)} %points_ref.3, f32[384,512]{1,0:T(8,128)} %prior_ref.3, s32[3,384]{1,0:T(4,128)} %active_ref.1, ...), custom_call_target="tpu_custom_call" | custom-call | tf_op jit(solution)/shard_map/window/pallas_call | solution.py:228
  78.3 0.0 copy-start.3
  78.3 0.7 copy-done.3
  79.0 0.6 reduce.1
Async XLA Ops:
  4.8 3.2 %collective-permute-start = (f32[192,768]{1,0:T(8,128)}, f32[192,768]{1,0:T(8,128)S(1)}, u32[]{:S(2)}, u32[]{:S(2)}) collective-permute-start(f32[192,768]{1,0:T(8,128)} %get-tuple-element.7), channel_id=1, source_target_pairs={{0,1},{1,0},{2,3},{3,2},{4,5},{5,4},{6,7},{7,6},{8,9},{9,8},{10,11... | collective-permute-start | bytes 1769480 | tf_op jit(solution)/shard_map/ppermute | solution.py:211
  8.0 0.8 %copy-start.1 = (f32[192,768]{1,0:T(8,128)}, f32[192,768]{1,0:T(8,128)S(1)}, u32[]{:S(2)}) copy-start(f32[192,768]{1,0:T(8,128)S(1)} %collective-permute-done.came_ref) | copy-start | bytes 1769476
  51.6 5.1 %copy-start = (f32[64,1,2304]{2,1,0:T(1,128)}, f32[64,1,2304]{2,1,0:T(1,128)S(1)}, u32[]{:S(2)}) copy-start(f32[64,1,2304]{2,1,0:T(1,128)S(1)} %all_to_all.11.mine_ref) | copy-start | bytes 1769476
  51.6 5.1 %collective-permute-start.1 = (f32[64,1,2304]{2,1,0:T(1,128)S(1)}, f32[64,1,2304]{2,1,0:T(1,128)S(1)}, u32[]{:S(2)}, u32[]{:S(2)}) collective-permute-start(f32[64,1,2304]{2,1,0:T(1,128)S(1)} %all_to_all.11.mine_ref), channel_id=1, source_target_pairs={{0,1},{1,0},{2,3},{3,2},{4,5},{5,4},{6,7},{7,6},{8,9},{9,8},{10,11... | collective-permute-start | bytes 1769480 | tf_op jit(solution)/shard_map/ppermute | solution.py:227
  56.7 0.8 %copy-start.2 = (f32[64,1,2304]{2,1,0:T(1,128)}, f32[64,1,2304]{2,1,0:T(1,128)S(1)}, u32[]{:S(2)}) copy-start(f32[64,1,2304]{2,1,0:T(1,128)S(1)} %collective-permute-done.1.other_ref) | copy-start | bytes 1769476
  78.3 0.7 copy-start.3

commit v2 on v1

v2 whole, which is shorter than its diff:
```python
import functools

import jax
import jax.numpy as jnp
from jax import lax
from jax.experimental import pallas as pl
from jax.experimental.pallas import tpu as pltpu
from jax.sharding import PartitionSpec as P

D = 256
R0 = 512
F = D + R0
PANEL = 128
PANELS = 3
PIV = PANEL * PANELS
HALF = PIV // 2
STRIP = 8
LOOK = 2
BF = jnp.bfloat16
F32 = jnp.float32
NT = (((1,), (1,)), ((), ()))
NN = (((1,), (0,)), ((), ()))


def split2(a):
    high = a.astype(BF)
    return high, (a - high.astype(F32)).astype(BF)


def split3(a):
    high = a.astype(BF)
    rest = a - high.astype(F32)
    mid = rest.astype(BF)
    return high, mid, (rest - mid.astype(F32)).astype(BF)


def dot_bf(a, b, dims=NT):
    return lax.dot_general(a, b, dims, preferred_element_type=F32)


def dot_x3(a, b, dims=NT):
    return three(split2(a), split2(b), dims)


def three(a, b, dims=NT):
    return dot_bf(a[0], b[0], dims) + (dot_bf(a[0], b[1], dims) + dot_bf(a[1], b[0], dims))


def six(a, b, dims=NT):
    small = dot_bf(a[0], b[2], dims) + dot_bf(a[1], b[1], dims) + dot_bf(a[2], b[0], dims)
    return dot_bf(a[0], b[0], dims) + (dot_bf(a[0], b[1], dims) + dot_bf(a[1], b[0], dims) + small)


def column_of(row):
    return jnp.transpose(jnp.broadcast_to(row, (8, 128)))[:, 0:1]


def pack_kernel(pivots_ref, points_ref, prior_ref, keep_ref, give_ref, all_ref):
    rows = points_ref.shape[0]
    index = lax.axis_index("rows")
    core = lax.rem(index, 2)
    base = (index * rows).astype(F32)
    lanes = lax.broadcasted_iota(jnp.int32, (PANEL, rows), 1).astype(F32)
    parts = [split3(points_ref[...]), split3(prior_ref[...])]
    for panel in range(PANELS):
        wanted = column_of(pivots_ref[panel : panel + 1, :].astype(F32)) - base
        select = (lanes == wanted).astype(BF)
        at = 0
        for high, mid, low in parts:
            got = dot_bf(select, high, NN) + dot_bf(select, mid, NN)
            got = got + dot_bf(select, low, NN)
            all_ref[panel * PANEL : (panel + 1) * PANEL, at : at + got.shape[1]] = got
            at += got.shape[1]
    keep_ref[...] = all_ref[pl.ds(pl.multiple_of(core * HALF, HALF), HALF), :]
    give_ref[...] = all_ref[pl.ds(pl.multiple_of((1 - core) * HALF, HALF), HALF), :]


def fold_kernel(keep_ref, came_ref, out_ref):
    homes = out_ref.shape[0]
    for turn in range(HALF // homes):
        span = pl.ds(turn * homes, homes)
        out_ref[:, 0, turn * F : (turn + 1) * F] = keep_ref[span, :] + came_ref[span, :]


def spread_lane(block, lane):
    return jnp.broadcast_to(block[:, lane : lane + 1], (STRIP, PANEL))


def spread_row(block, row):
    return jnp.broadcast_to(block[row : row + 1, :], (STRIP, PANEL))


def factor(w_ref, z_ref, inv_ref):
    size = PANEL
    strips = size // STRIP
    iota = lax.broadcasted_iota(jnp.int32, (STRIP, size), 0)
    z_ref[...] = jnp.zeros_like(z_ref)
    left, right, ready = {}, {}, {}
    for strip in range(strips):
        first = STRIP * strip
        after = first + STRIP
        groups = range(min(LOOK + 1, strips - strip))
        for group in groups:
            if strip + group not in left:
                rows = slice(first + STRIP * group, after + STRIP * group)
                left[strip + group] = w_ref[rows, 0:size]
                right[strip + group] = w_ref[rows, size : 2 * size]
        column = {}
        for group in groups:
            for j in range(STRIP):
                if group == 0 and strip > 0:
                    column[group, j] = ready[j]
                else:
                    column[group, j] = spread_lane(left[strip + group], first + j)
        ready = {}
        if strip + 1 < strips:
            ready = {m: spread_lane(left[strip + 1], after + m) for m in range(STRIP)}
        for j in range(STRIP):
            root = lax.rsqrt(spread_row(column[0, j], j))
            inverse = root * root
            row_left = spread_row(left[strip], j)
            row_right = spread_row(right[strip], j)
            inv_ref[first + j : first + j + 1, :] = row_right[0:1] * root[0:1]
            own = {m: spread_row(column[0, m], j) for m in range(j + 1, STRIP)}
            ahead = {m: spread_row(column[1, j], m) for m in ready}
            for group in groups:
                weight = column[group, j] * inverse
                if group == 0:
                    weight = jnp.where(iota == j, 1.0 - inverse, weight)
                for m in own:
                    column[group, m] = column[group, m] - weight * own[m]
                if group == 1:
                    for m in ready:
                        ready[m] = ready[m] - weight * ahead[m]
                left[strip + group] = left[strip + group] - weight * row_left
                right[strip + group] = right[strip + group] - weight * row_right
        last = first + STRIP * (LOOK + 1)
        if last < size:
            if strip > 0:
                z_ref[first - STRIP : first, :] = jnp.zeros((STRIP, 2 * size), F32)
            z_ref[first:after, 0:size] = left[strip]
            z_ref[first:after, size : 2 * size] = right[strip]
            update = dot_x3(w_ref[last:size, 0:size], z_ref[...], NN)
            w_ref[last:size, :] = w_ref[last:size, :] - update


def row_of(column):
    return jnp.transpose(jnp.broadcast_to(column, (PANEL, PANEL)))[0:1, :]


def window_kernel(
    noise_ref,
    pivots_ref,
    scale_ref,
    active_ref,
    mine_hbm,
    other_hbm,
    points_hbm,
    prior_hbm,
    new_hbm,
    diag_ref,
    mine_ref,
    other_ref,
    points_ref,
    prior_ref,
    pp_ref,
    pf_ref,
    k_ref,
    w_ref,
    z_ref,
    inv_ref,
    x_ref,
    sems,
    out_sems,
):
    loads = [
        pltpu.make_async_copy(source, target, sems.at[i])
        for i, (source, target) in enumerate(
            (
                (mine_hbm, mine_ref),
                (other_hbm, other_ref),
                (points_hbm, points_ref),
                (prior_hbm, prior_ref),
            )
        )
    ]
    for load in loads:
        load.start()
    rows = points_ref.shape[0]
    homes = mine_ref.shape[0]
    index = lax.axis_index("rows")
    core = lax.rem(index, 2)
    base = index * rows
    noise = noise_ref[0]
    scale = scale_ref[...]
    for load, ref, half in ((loads[0], mine_ref, core), (loads[1], other_ref, 1 - core)):
        load.wait()
        for turn in range(HALF // homes):
            at = pl.ds(pl.multiple_of(half * HALF, HALF) + turn * homes, homes)
            pp_ref[at, :] = ref[:, 0, turn * F : turn * F + D] * scale
            pf_ref[at, :] = ref[:, 0, turn * F + D : (turn + 1) * F]
    pp = pp_ref[...]
    pp3 = split3(pp)
    pf2 = split2(pf_ref[...])
    square_col = jnp.sum(pp * pp, axis=1, keepdims=True)
    square_row = jnp.concatenate(
        [row_of(square_col[i * PANEL : (i + 1) * PANEL]) for i in range(PANELS)], axis=1
    )
    eye = (
        lax.broadcasted_iota(jnp.int32, (PIV, PIV), 0)
        == lax.broadcasted_iota(jnp.int32, (PIV, PIV), 1)
    ).astype(F32)
    gram = jnp.exp(-0.5 * (square_col + square_row - 2.0 * six(pp3, pp3))) + noise * eye
    k_ref[...] = gram - three(pf2, pf2)
    loads[2].wait()
    loads[3].wait()
    mine = points_ref[...] * scale
    prior = prior_ref[...]
    mine_col = jnp.sum(mine * mine, axis=1, keepdims=True)
    residual = jnp.exp(-0.5 * (mine_col + square_row - 2.0 * six(split3(mine), pp3)))
    residual = residual - three(split2(prior), pf2)
    ids = base + lax.broadcasted_iota(jnp.int32, (rows, PANEL), 0)
    for panel in range(PANELS):
        span = slice(panel * PANEL, (panel + 1) * PANEL)
        same = (ids == pivots_ref[panel : panel + 1, :]).astype(F32)
        x_ref[:, span] = residual[:, span] + noise * same
    small_eye = eye[0:PANEL, 0:PANEL]
    total = jnp.sum(prior * prior, axis=1, keepdims=True)
    stores = []
    for panel in range(PANELS):
        span = slice(panel * PANEL, (panel + 1) * PANEL)
        w_ref[:, 0:PANEL] = k_ref[span, span]
        w_ref[:, PANEL:] = small_eye
        factor(w_ref, z_ref, inv_ref)
        inverse = split2(inv_ref[...])
        if panel + 1 < PANELS:
            rest = slice((panel + 1) * PANEL, PIV)
            below = split2(three(split2(k_ref[rest, span]), inverse))
            k_ref[rest, rest] = k_ref[rest, rest] - three(below, below)
        fresh = three(split2(x_ref[:, span]), inverse)
        mask = jnp.concatenate(
            [
                column_of(active_ref[panel : panel + 1, i * 128 : (i + 1) * 128].astype(F32))
                for i in range(rows // 128)
            ],
            axis=0,
        )
        fresh = fresh * mask
        x_ref[:, span] = fresh
        store = pltpu.make_async_copy(x_ref.at[:, span], new_hbm.at[:, span], out_sems.at[panel])
        store.start()
        stores.append(store)
        total = total + jnp.sum(fresh * fresh, axis=1, keepdims=True)
        if panel + 1 < PANELS:
            x_ref[:, rest] = x_ref[:, rest] - three(split2(fresh), below)
    diag = (1.0 + noise) - total
    for i in range(rows // 128):
        diag_ref[:, i * 128 : (i + 1) * 128] = row_of(diag[i * 128 : (i + 1) * 128])
    for store in stores:
        store.wait()


SMEM = pl.BlockSpec(memory_space=pltpu.SMEM)
VMEM = pl.BlockSpec(memory_space=pltpu.VMEM)
ANY = pl.BlockSpec(memory_space=pl.ANY)


def local(points, inv_scale, noise, prior, active, pivots):
    rows = points.shape[0]
    devices = lax.axis_size("rows")
    homes = devices // 2
    partner = [(i, i ^ 1) for i in range(devices)]
    groups = [[2 * chip + core for chip in range(homes)] for core in range(2)]
    half = jax.ShapeDtypeStruct((HALF, F), F32)
    keep, give = pl.pallas_call(
        pack_kernel,
        out_shape=(half, half),
        in_specs=[VMEM, VMEM, VMEM],
        out_specs=(VMEM, VMEM),
        scratch_shapes=[pltpu.VMEM((PIV, F), F32)],
        name="pack",
    )(pivots, points, prior)
    came = lax.ppermute(give, "rows", partner)
    wide = jax.ShapeDtypeStruct((homes, 1, HALF // homes * F), F32)
    spread = pl.pallas_call(
        fold_kernel, out_shape=wide, in_specs=[VMEM, VMEM], out_specs=VMEM, name="fold"
    )(keep, came)
    exchange = functools.partial(
        lax.all_to_all,
        axis_name="rows",
        split_axis=0,
        concat_axis=0,
        axis_index_groups=groups,
        tiled=True,
    )
    got = exchange(spread)
    owned = jnp.broadcast_to(jnp.sum(got, axis=0, keepdims=True), wide.shape)
    mine = exchange(owned)
    other = lax.ppermute(mine, "rows", partner)
    new, diag = pl.pallas_call(
        window_kernel,
        out_shape=(
            jax.ShapeDtypeStruct((rows, PIV), F32),
            jax.ShapeDtypeStruct((1, rows), F32),
        ),
        in_specs=[SMEM, VMEM, VMEM, VMEM] + [ANY] * 4,
        out_specs=(ANY, VMEM),
        scratch_shapes=[
            pltpu.VMEM(wide.shape, F32),
            pltpu.VMEM(wide.shape, F32),
            pltpu.VMEM((rows, D), F32),
            pltpu.VMEM((rows, R0), F32),
            pltpu.VMEM((PIV, D), F32),
            pltpu.VMEM((PIV, R0), F32),
            pltpu.VMEM((PIV, PIV), F32),
            pltpu.VMEM((PANEL, 2 * PANEL), F32),
            pltpu.VMEM((PANEL, 2 * PANEL), F32),
            pltpu.VMEM((PANEL, PANEL), F32),
            pltpu.VMEM((rows, PIV), F32),
            pltpu.SemaphoreType.DMA((4,)),
            pltpu.SemaphoreType.DMA((PANELS,)),
        ],
        name="window",
    )(noise, pivots, inv_scale.reshape(1, D), active, mine, other, points, prior)
    return (new, diag.reshape(rows))


def solution(mesh):
    return jax.shard_map(
        local,
        mesh=mesh,
        in_specs=(P("rows", None), P(), P(), P("rows", None), P(None, "rows"), P()),
        out_specs=(P("rows", None), P("rows")),
        check_vma=False,
    )
```

time: 79.9 us -> 74.5 us (0.932)
  Pallas kernels: 26.6 us -> 21.7 us
    pallas_call x1, Pallas kernels: 20.8 us -> 15.8 us  [local(): pl.pallas_call(window_kernel, out_shape=(jax.ShapeDtypeStruct((rows, PIV)...]
where the time goes in v2:
time: 74.5 us; the launch traced here: 74.1 us
  blocking collectives  39.9 us (54%)
  Pallas kernels  21.7 us (29%)
  starting transfers between devices  4.79 us (6%)
  waiting for transfers between devices  2.82 us (4%)
  local copies, waits for them, and re-layouts  2.59 us (3%)
  between operations  1.31 us (2%)
  other arithmetic  0.95 us (1%)
    all_to_all x1, blocking collectives, local(): got = exchange(spread)  23.9 us
    all_to_all x1, blocking collectives, local(): mine = exchange(owned)  16 us
    pallas_call x1, Pallas kernels, local(): pl.pallas_call(window_kernel, out_shape=(jax.ShapeDtypeStruct((rows, PIV)...  15.8 us
    pallas_call x1, Pallas kernels, local(): pl.pallas_call(pack_kernel, out_shape=(half, half), in_specs=[VMEM, VMEM,...  3.71 us
    ppermute x1, starting transfers between devices, local(): other = lax.ppermute(mine, 'rows', partner)  3.43 us
    unnamed x8, local copies, waits for them, and re-layouts  2.29 us
    pallas_call x1, Pallas kernels, local(): pl.pallas_call(fold_kernel, out_shape=wide, in_specs=[VMEM, VMEM], out_sp...  2.19 us
    ppermute x1, waiting for transfers between devices, local(): came = lax.ppermute(give, 'rows', partner)  1.84 us
  transfers between devices with their start and end apart: 2, of which 2 were waited for; matrix products, arithmetic and copies ran while one was open for 0% of the time, Pallas kernels for 0%

profile of v2, /device:TPU:1, one launch (start us, length us, event | category | flops | bytes accessed | tf_op | source)
XLA Modules:
  0.0 74.1 jit_solution(6635820525361311465)
XLA Ops:
  0.6 3.7 %pack.1 = (f32[192,768]{1,0:T(8,128)}, f32[192,768]{1,0:T(8,128)}) custom-call(s32[3,128]{1,0:T(4,128)} %pivots_ref.3, f32[384,256]{1,0:T(8,128)} %points_hbm.1, f32[384,512]{1,0:T(8,128)} %prior_hbm.1), custom_call_target="tpu_custom_call" | custom-call | tf_op jit(solution)/shard_map/pack/pallas_call | solution.py:275
  4.3 1.4 %collective-permute-start = (f32[192,768]{1,0:T(8,128)}, f32[192,768]{1,0:T(8,128)S(1)}, u32[]{:S(2)}, u32[]{:S(2)}) collective-permute-start(f32[192,768]{1,0:T(8,128)} %get-tuple-element.7), channel_id=1, source_target_pairs={{0,1},{1,0},{2,3},{3,2},{4,5},{5,4},{6,7},{7,6},{8,9},{9,8},{10,11... | collective-permute-start | bytes 1769480 | tf_op jit(solution)/shard_map/ppermute | solution.py:283
  5.7 1.8 %collective-permute-done.came_ref = f32[192,768]{1,0:T(8,128)S(1)} collective-permute-done((f32[192,768]{1,0:T(8,128)}, f32[192,768]{1,0:T(8,128)S(1)}, u32[]{:S(2)}, u32[]{:S(2)}) %collective-permute-start) | collective-permute-done | bytes 589856 | tf_op jit(solution)/shard_map/ppermute | solution.py:283
  7.5 0.0 copy-start.1
  7.5 0.8 %copy-done.1 = f32[192,768]{1,0:T(8,128)} copy-done((f32[192,768]{1,0:T(8,128)}, f32[192,768]{1,0:T(8,128)S(1)}, u32[]{:S(2)}) %copy-start.1) | copy-done | bytes 589848
  8.4 2.2 %fold.1 = f32[64,1,2304]{2,1,0:T(1,128)} custom-call(f32[192,768]{1,0:T(8,128)} %get-tuple-element.6.keep_ref, f32[192,768]{1,0:T(8,128)} %copy-done.1), custom_call_target="tpu_custom_call" | custom-call | tf_op jit(solution)/shard_map/fold/pallas_call | solution.py:285
  10.5 23.9 %all_to_all.10 = f32[64,1,2304]{2,1,0:T(1,128)S(1)} all-to-all(f32[64,1,2304]{2,1,0:T(1,128)} %fold.1), channel_id=1, replica_groups={{0,2,4,6,8,10,12,14,16,18,20,22,24,26,28,30,32,34,36,38,40,42,44,46,48,..., dimensions={0} | all-to-all | bytes 1179648 | tf_op jit(solution)/shard_map/all_to_all | solution.py:296
  34.4 0.4 reduce_sum.9
  34.8 0.3 broadcast_in_dim.2
  35.1 16.0 %all_to_all.11.mine_hbm = f32[64,1,2304]{2,1,0:T(1,128)S(1)} all-to-all(f32[64,1,2304]{2,1,0:T(1,128)S(1)} %broadcast_in_dim.2), channel_id=1, replica_groups={{0,2,4,6,8,10,12,14,16,18,20,22,24,26,28,30,32,34,36,38,40,42,44,46,48,..., dimensions={0} | all-to-all | bytes 1179648 | tf_op jit(solution)/shard_map/all_to_all | solution.py:298
  51.1 0.0 copy-start
  51.1 3.4 %collective-permute-start.1 = (f32[64,1,2304]{2,1,0:T(1,128)S(1)}, f32[64,1,2304]{2,1,0:T(1,128)S(1)}, u32[]{:S(2)}, u32[]{:S(2)}) collective-permute-start(f32[64,1,2304]{2,1,0:T(1,128)S(1)} %all_to_all.11.mine_hbm), channel_id=1, source_target_pairs={{0,1},{1,0},{2,3},{3,2},{4,5},{5,4},{6,7},{7,6},{8,9},{9,8},{10,11... | collective-permute-start | bytes 1769480 | tf_op jit(solution)/shard_map/ppermute | solution.py:299
  55.2 1.0 %collective-permute-done.1.other_hbm = f32[64,1,2304]{2,1,0:T(1,128)S(1)} collective-permute-done((f32[64,1,2304]{2,1,0:T(1,128)S(1)}, f32[64,1,2304]{2,1,0:T(1,128)S(1)}, u32[]{:S(2)}, u32[]{:S(2)}) %collective-permute-start.1) | collective-permute-done | bytes 589856 | tf_op jit(solution)/shard_map/ppermute | solution.py:299
  56.2 0.0 copy-start.2
  56.2 0.0 copy-done
  56.2 0.8 %copy-done.2 = f32[64,1,2304]{2,1,0:T(1,128)} copy-done((f32[64,1,2304]{2,1,0:T(1,128)}, f32[64,1,2304]{2,1,0:T(1,128)S(1)}, u32[]{:S(2)}) %copy-start.2) | copy-done | bytes 589848
  57.0 15.8 %window.1 = (f32[384,384]{1,0:T(8,128)}, f32[1,384]{1,0:T(1,128)}) custom-call(f32[1]{0:T(128)S(6)} %copy.8.noise_ref, s32[3,128]{1,0:T(4,128)} %pivots_ref.3, f32[1,256]{1,0:T(1,128)} %bitcast.1, s32[3,384]{1,0:T(4,128)} %active_ref.1, f32[64,1,2304]{2,1,0:T(1,128)} %copy-done, f32[64,1,2304]{2,1,0:T(1,128)} %copy-done.2, f32[384,256]{1,0:T(8,128)} %points_hbm.1, ...), custom_call_target="tpu_custom_call" | custom-call | tf_op jit(solution)/shard_map/window/pallas_call | solution.py:300
  72.8 0.0 copy-start.3
  72.8 0.7 copy-done.3
  73.5 0.6 reduce.1
Async XLA Ops:
  4.3 3.2 %collective-permute-start = (f32[192,768]{1,0:T(8,128)}, f32[192,768]{1,0:T(8,128)S(1)}, u32[]{:S(2)}, u32[]{:S(2)}) collective-permute-start(f32[192,768]{1,0:T(8,128)} %get-tuple-element.7), channel_id=1, source_target_pairs={{0,1},{1,0},{2,3},{3,2},{4,5},{5,4},{6,7},{7,6},{8,9},{9,8},{10,11... | collective-permute-start | bytes 1769480 | tf_op jit(solution)/shard_map/ppermute | solution.py:283
  7.5 0.8 %copy-start.1 = (f32[192,768]{1,0:T(8,128)}, f32[192,768]{1,0:T(8,128)S(1)}, u32[]{:S(2)}) copy-start(f32[192,768]{1,0:T(8,128)S(1)} %collective-permute-done.came_ref) | copy-start | bytes 1769476
  51.1 5.1 %copy-start = (f32[64,1,2304]{2,1,0:T(1,128)}, f32[64,1,2304]{2,1,0:T(1,128)S(1)}, u32[]{:S(2)}) copy-start(f32[64,1,2304]{2,1,0:T(1,128)S(1)} %all_to_all.11.mine_hbm) | copy-start | bytes 1769476
  51.1 5.1 %collective-permute-start.1 = (f32[64,1,2304]{2,1,0:T(1,128)S(1)}, f32[64,1,2304]{2,1,0:T(1,128)S(1)}, u32[]{:S(2)}, u32[]{:S(2)}) collective-permute-start(f32[64,1,2304]{2,1,0:T(1,128)S(1)} %all_to_all.11.mine_hbm), channel_id=1, source_target_pairs={{0,1},{1,0},{2,3},{3,2},{4,5},{5,4},{6,7},{7,6},{8,9},{9,8},{10,11... | collective-permute-start | bytes 1769480 | tf_op jit(solution)/shard_map/ppermute | solution.py:299
  56.2 0.8 %copy-start.2 = (f32[64,1,2304]{2,1,0:T(1,128)}, f32[64,1,2304]{2,1,0:T(1,128)S(1)}, u32[]{:S(2)}) copy-start(f32[64,1,2304]{2,1,0:T(1,128)S(1)} %collective-permute-done.1.other_hbm) | copy-start | bytes 1769476
  72.8 0.7 copy-start.3

commit v3 on v2

--- a/solution.py
+++ b/solution.py
@@ -55,31 +55,67 @@
     return jnp.transpose(jnp.broadcast_to(row, (8, 128)))[:, 0:1]
 
 
-def pack_kernel(pivots_ref, points_ref, prior_ref, keep_ref, give_ref, all_ref):
+def pivot_columns(pivots_ref):
+    return [column_of(pivots_ref[p : p + 1, :].astype(F32)) for p in range(PANELS)]
+
+
+def pivot_order(pivots_ref):
+    smaller = []
+    for column in pivot_columns(pivots_ref):
+        ahead = [
+            (pivots_ref[p : p + 1, :].astype(F32) < column).astype(F32) for p in range(PANELS)
+        ]
+        smaller.append(jnp.sum(ahead[0] + ahead[1] + ahead[2], axis=1, keepdims=True))
+    return jnp.concatenate(smaller, axis=0)
+
+
+def count_rows(tests):
+    total = tests[0].astype(F32)
+    for test in tests[1:]:
+        total = total + test.astype(F32)
+    return jnp.sum(total, axis=0, keepdims=True)
+
+
+def pack_kernel(turn_ref, pivots_ref, points_ref, prior_ref, send_ref, pick_ref, turns_ref):
     rows = points_ref.shape[0]
+    devices = send_ref.shape[0]
     index = lax.axis_index("rows")
-    core = lax.rem(index, 2)
+    turn = turn_ref[0].astype(F32)
     base = (index * rows).astype(F32)
-    lanes = lax.broadcasted_iota(jnp.int32, (PANEL, rows), 1).astype(F32)
-    parts = [split3(points_ref[...]), split3(prior_ref[...])]
-    for panel in range(PANELS):
-        wanted = column_of(pivots_ref[panel : panel + 1, :].astype(F32)) - base
-        select = (lanes == wanted).astype(BF)
-        at = 0
-        for high, mid, low in parts:
-            got = dot_bf(select, high, NN) + dot_bf(select, mid, NN)
-            got = got + dot_bf(select, low, NN)
-            all_ref[panel * PANEL : (panel + 1) * PANEL, at : at + got.shape[1]] = got
-            at += got.shape[1]
-    keep_ref[...] = all_ref[pl.ds(pl.multiple_of(core * HALF, HALF), HALF), :]
-    give_ref[...] = all_ref[pl.ds(pl.multiple_of((1 - core) * HALF, HALF), HALF), :]
-
-
-def fold_kernel(keep_ref, came_ref, out_ref):
-    homes = out_ref.shape[0]
-    for turn in range(HALF // homes):
-        span = pl.ds(turn * homes, homes)
-        out_ref[:, 0, turn * F : (turn + 1) * F] = keep_ref[span, :] + came_ref[span, :]
+    columns = pivot_columns(pivots_ref)
+    ids = base + lax.broadcasted_iota(jnp.int32, (1, rows), 1).astype(F32)
+    place = count_rows([column < ids for column in columns])
+    found = count_rows([column == ids for column in columns])
+    step = place - place[:, 0:1] - devices * turn
+    home = place - devices * jnp.floor(place * (1.0 / devices))
+    home = jnp.where((found > 0.5) & (step >= 0.0) & (step < devices), home, -1.0)
+    target = lax.broadcasted_iota(jnp.int32, (devices, rows), 0).astype(F32)
+    select = (target == home).astype(BF)
+    at = 0
+    for ref in (points_ref, prior_ref):
+        high, mid, low = split3(ref[...])
+        got = dot_bf(select, high, NN) + dot_bf(select, mid, NN) + dot_bf(select, low, NN)
+        send_ref[:, 0, at : at + got.shape[1]] = got
+        at += got.shape[1]
+    edges = rows * lax.broadcasted_iota(jnp.int32, (1, devices), 1).astype(F32)
+    start = count_rows([column < edges for column in columns])
+    stop = count_rows([column < edges + rows for column in columns])
+    slot = lax.broadcasted_iota(jnp.int32, (8, devices), 0)
+    wanted = index.astype(F32) + devices * slot.astype(F32)
+    step = wanted - start - devices * turn
+    pick = (wanted >= start) & (wanted < stop) & (step >= 0.0) & (step < devices)
+    pick_ref[...] = (pick & (slot < PIV // devices)).astype(F32)
+    longest = jnp.max(stop - start)
+    turns_ref[0] = jnp.where(longest > 2 * devices, 3, jnp.where(longest > devices, 2, 1))
+
+
+def pick_kernel(pick_ref, came_ref, out_ref, rows_ref):
+    rows_ref[...] = came_ref[:, 0, :]
+    select = pick_ref[...].astype(BF)
+    high, mid, low = split3(rows_ref[...])
+    got = dot_bf(select, high, NN) + dot_bf(select, mid, NN) + dot_bf(select, low, NN)
+    for row in range(out_ref.shape[2] // F):
+        out_ref[0, :, row * F : (row + 1) * F] = got[row : row + 1, :]
 
 
 def spread_lane(block, lane):
@@ -153,39 +189,20 @@
     pivots_ref,
     scale_ref,
     active_ref,
-    mine_hbm,
-    other_hbm,
-    points_hbm,
-    prior_hbm,
-    new_hbm,
-    diag_ref,
     mine_ref,
     other_ref,
     points_ref,
     prior_ref,
-    pp_ref,
-    pf_ref,
+    new_hbm,
+    diag_ref,
+    g_ref,
     k_ref,
     w_ref,
     z_ref,
     inv_ref,
     x_ref,
-    sems,
     out_sems,
 ):
-    loads = [
-        pltpu.make_async_copy(source, target, sems.at[i])
-        for i, (source, target) in enumerate(
-            (
-                (mine_hbm, mine_ref),
-                (other_hbm, other_ref),
-                (points_hbm, points_ref),
-                (prior_hbm, prior_ref),
-            )
-        )
-    ]
-    for load in loads:
-        load.start()
     rows = points_ref.shape[0]
     homes = mine_ref.shape[0]
     index = lax.axis_index("rows")
@@ -193,15 +210,19 @@
     base = index * rows
     noise = noise_ref[0]
     scale = scale_ref[...]
-    for load, ref, half in ((loads[0], mine_ref, core), (loads[1], other_ref, 1 - core)):
-        load.wait()
+    for ref, half in ((mine_ref, core), (other_ref, 1 - core)):
         for turn in range(HALF // homes):
             at = pl.ds(pl.multiple_of(half * HALF, HALF) + turn * homes, homes)
-            pp_ref[at, :] = ref[:, 0, turn * F : turn * F + D] * scale
-            pf_ref[at, :] = ref[:, 0, turn * F + D : (turn + 1) * F]
-    pp = pp_ref[...]
-    pp3 = split3(pp)
-    pf2 = split2(pf_ref[...])
+            g_ref[at, :] = ref[:, 0, turn * F : (turn + 1) * F]
+    order = pivot_order(pivots_ref)
+    lane = lax.broadcasted_iota(jnp.int32, (1, PIV), 1)
+    half, turn, home = lane // HALF, lane % HALF // homes, lane % homes
+    held = (2 * home + half + 2 * homes * turn).astype(F32)
+    place = (order == held).astype(BF)
+    pp3 = [dot_bf(place, part, NN) for part in split3(g_ref[:, 0:D] * scale)]
+    pp = pp3[0] + pp3[1] + pp3[2]
+    pp3 = [part.astype(BF) for part in pp3]
+    pf2 = [dot_bf(place, part, NN).astype(BF) for part in split2(g_ref[:, D:F])]
     square_col = jnp.sum(pp * pp, axis=1, keepdims=True)
     square_row = jnp.concatenate(
         [row_of(square_col[i * PANEL : (i + 1) * PANEL]) for i in range(PANELS)], axis=1
@@ -212,8 +233,6 @@
     ).astype(F32)
     gram = jnp.exp(-0.5 * (square_col + square_row - 2.0 * six(pp3, pp3))) + noise * eye
     k_ref[...] = gram - three(pf2, pf2)
-    loads[2].wait()
-    loads[3].wait()
     mine = points_ref[...] * scale
     prior = prior_ref[...]
     mine_col = jnp.sum(mine * mine, axis=1, keepdims=True)
@@ -255,13 +274,14 @@
             x_ref[:, rest] = x_ref[:, rest] - three(split2(fresh), below)
     diag = (1.0 + noise) - total
     for i in range(rows // 128):
-        diag_ref[:, i * 128 : (i + 1) * 128] = row_of(diag[i * 128 : (i + 1) * 128])
+        diag_ref[i * 128 : (i + 1) * 128] = row_of(diag[i * 128 : (i + 1) * 128])[0]
     for store in stores:
         store.wait()
 
 
 SMEM = pl.BlockSpec(memory_space=pltpu.SMEM)
 VMEM = pl.BlockSpec(memory_space=pltpu.VMEM)
+SMALL = pltpu.CompilerParams(vmem_limit_bytes=16 * 1024 * 1024)
 ANY = pl.BlockSpec(memory_space=pl.ANY)
 
 
@@ -271,58 +291,65 @@
     homes = devices // 2
     partner = [(i, i ^ 1) for i in range(devices)]
     groups = [[2 * chip + core for chip in range(homes)] for core in range(2)]
-    half = jax.ShapeDtypeStruct((HALF, F), F32)
-    keep, give = pl.pallas_call(
-        pack_kernel,
-        out_shape=(half, half),
-        in_specs=[VMEM, VMEM, VMEM],
-        out_specs=(VMEM, VMEM),
-        scratch_shapes=[pltpu.VMEM((PIV, F), F32)],
-        name="pack",
-    )(pivots, points, prior)
-    came = lax.ppermute(give, "rows", partner)
-    wide = jax.ShapeDtypeStruct((homes, 1, HALF // homes * F), F32)
-    spread = pl.pallas_call(
-        fold_kernel, out_shape=wide, in_specs=[VMEM, VMEM], out_specs=VMEM, name="fold"
-    )(keep, came)
     exchange = functools.partial(
-        lax.all_to_all,
-        axis_name="rows",
-        split_axis=0,
-        concat_axis=0,
-        axis_index_groups=groups,
-        tiled=True,
+        lax.all_to_all, axis_name="rows", split_axis=0, concat_axis=0, tiled=True
     )
-    got = exchange(spread)
-    owned = jnp.broadcast_to(jnp.sum(got, axis=0, keepdims=True), wide.shape)
-    mine = exchange(owned)
+    def routed(turn):
+        send, pick, turns = pl.pallas_call(
+            pack_kernel,
+            out_shape=(
+                jax.ShapeDtypeStruct((devices, 1, F), F32),
+                jax.ShapeDtypeStruct((8, devices), F32),
+                jax.ShapeDtypeStruct((1,), jnp.int32),
+            ),
+            in_specs=[SMEM, VMEM, VMEM, VMEM],
+            out_specs=(VMEM, VMEM, SMEM),
+            name="pack",
+            compiler_params=SMALL,
+        )(turn, pivots, points, prior)
+        owned = pl.pallas_call(
+            pick_kernel,
+            out_shape=jax.ShapeDtypeStruct((1, 1, PIV // devices * F), F32),
+            in_specs=[VMEM, VMEM],
+            out_specs=VMEM,
+            scratch_shapes=[pltpu.VMEM((devices, F), F32)],
+            name="pick",
+            compiler_params=SMALL,
+        )(pick, exchange(send))
+        return owned, turns[0]
+
+    owned, turns = routed(jnp.zeros((1,), jnp.int32))
+
+    def more(state):
+        return state[0] < turns
+
+    def again(state):
+        turn, owned = state
+        return turn + 1, owned + routed(turn[None])[0]
+
+    owned = lax.while_loop(more, again, (jnp.int32(1), owned))[1]
+    mine = exchange(jnp.broadcast_to(owned, (homes, *owned.shape[1:])), axis_index_groups=groups)
     other = lax.ppermute(mine, "rows", partner)
-    new, diag = pl.pallas_call(
+    return pl.pallas_call(
         window_kernel,
         out_shape=(
             jax.ShapeDtypeStruct((rows, PIV), F32),
-            jax.ShapeDtypeStruct((1, rows), F32),
+            jax.ShapeDtypeStruct((rows,), F32),
         ),
-        in_specs=[SMEM, VMEM, VMEM, VMEM] + [ANY] * 4,
+        in_specs=[SMEM] + [VMEM] * 7,
         out_specs=(ANY, VMEM),
         scratch_shapes=[
-            pltpu.VMEM(wide.shape, F32),
-            pltpu.VMEM(wide.shape, F32),
-            pltpu.VMEM((rows, D), F32),
-            pltpu.VMEM((rows, R0), F32),
-            pltpu.VMEM((PIV, D), F32),
-            pltpu.VMEM((PIV, R0), F32),
+            pltpu.VMEM((PIV, F), F32),
             pltpu.VMEM((PIV, PIV), F32),
             pltpu.VMEM((PANEL, 2 * PANEL), F32),
             pltpu.VMEM((PANEL, 2 * PANEL), F32),
             pltpu.VMEM((PANEL, PANEL), F32),
             pltpu.VMEM((rows, PIV), F32),
-            pltpu.SemaphoreType.DMA((4,)),
             pltpu.SemaphoreType.DMA((PANELS,)),
         ],
         name="window",
+        compiler_params=SMALL,
     )(noise, pivots, inv_scale.reshape(1, D), active, mine, other, points, prior)
-    return (new, diag.reshape(rows))
 
 
 def solution(mesh):

time: 74.5 us -> 66.2 us (0.89)
  blocking collectives: 39.9 us -> 17.3 us
  waiting for transfers between devices: 2.82 us -> 13.1 us
  starting transfers between devices: 4.79 us -> 14 us
  Pallas kernels: 21.7 us -> 18.4 us
  local copies, waits for them, and re-layouts: 2.59 us -> 1 us
  other arithmetic: 0.95 us -> 0.03 us
    all_to_all x2 -> x1, blocking collectives: 39.9 us -> 17.3 us  [local(): exchange(jnp.broadcast_to(owned, (homes, *owned.shape[1:])), axis_index_g...]
    all_to_all x0 -> x1, waiting for transfers between devices: none -> 12.1 us  [routed(): exchange(send)]
    all_to_all x0 -> x1, starting transfers between devices: none -> 11.5 us  [routed(): exchange(send)]
    pallas_call x2, Pallas kernels: 5.9 us -> 3.22 us  [the longest x1 2.94 us: routed(): pl.pallas_call(pack_kernel, out_shape=(jax.ShapeDtypeStruct((devices, 1,...]
    ppermute x1 -> x0, waiting for transfers between devices: 1.84 us -> none  [local(): came = lax.ppermute(give, 'rows', partner)]
    unnamed x8 -> x10, local copies, waits for them, and re-layouts: 2.29 us -> 0.69 us
    ppermute x1 -> x0, starting transfers between devices: 1.36 us -> none  [local(): came = lax.ppermute(give, 'rows', partner)]
    ppermute x1, starting transfers between devices: 3.43 us -> 2.46 us  [local(): other = lax.ppermute(mine, 'rows', partner)]
where the time goes in v3:
time: 66.2 us; the launch traced here: 65.9 us
  Pallas kernels  18.4 us (28%)
  blocking collectives  17.3 us (26%)
  starting transfers between devices  14 us (21%)
  waiting for transfers between devices  13.1 us (20%)
  between operations  1.54 us (2%)
  local copies, waits for them, and re-layouts  1 us (2%)
    all_to_all x1, blocking collectives, local(): exchange(jnp.broadcast_to(owned, (homes, *owned.shape[1:])), axis_index_g...  17.3 us
    pallas_call x1, Pallas kernels, local(): pl.pallas_call(window_kernel, out_shape=(jax.ShapeDtypeStruct((rows, PIV)...  15.2 us
    all_to_all x1, waiting for transfers between devices, routed(): exchange(send)  12.1 us
    all_to_all x1, starting transfers between devices, routed(): exchange(send)  11.5 us
    pallas_call x1, Pallas kernels, routed(): pl.pallas_call(pack_kernel, out_shape=(jax.ShapeDtypeStruct((devices, 1,...  2.94 us
    ppermute x1, starting transfers between devices, local(): other = lax.ppermute(mine, 'rows', partner)  2.46 us
  transfers between devices with their start and end apart: 2, of which 2 were waited for; matrix products, arithmetic and copies ran while one was open for 0% of the time, Pallas kernels for 0%

profile of v3, /device:TPU:1, one launch (start us, length us, event | category | flops | bytes accessed | tf_op | source)
XLA Modules:
  0.0 65.9 jit_solution(14335043140487690672)
XLA Ops:
  0.6 2.9 %pack.2 = (f32[128,1,768]{2,1,0:T(1,128)}, f32[8,128]{1,0:T(8,128)S(1)}, s32[1]{0:T(128)}) custom-call(s32[1]{0:T(128)} %constant.2.clone.1.turn_ref, s32[3,128]{1,0:T(4,128)} %pivots_ref.3, f32[384,256]{1,0:T(8,128)} %points_ref.3, f32[384,512]{1,0:T(8,128)} %prior_ref.3), custom_call_target="tpu_custom_call" | custom-call | tf_op jit(solution)/shard_map/pack/pallas_call | solution.py:298
  3.6 0.0 copy-start.2
  3.6 11.5 %all-to-all-start.1 = ((f32[128,1,768]{2,1,0:T(1,128)}), f32[128,1,768]{2,1,0:T(1,128)S(1)}, u32[]{:S(2)}, u32[]{:S(2)}) async-start(f32[128,1,768]{2,1,0:T(1,128)} %get-tuple-element.41), calls=%async_computation.1 | async-start | bytes 786432 | tf_op jit(solution)/shard_map/all_to_all | solution.py:318
  15.1 0.0 copy-start.3
  15.1 12.1 %all-to-all-done.1.came_ref = f32[128,1,768]{2,1,0:T(1,128)S(1)} async-done(((f32[128,1,768]{2,1,0:T(1,128)}), f32[128,1,768]{2,1,0:T(1,128)S(1)}, u32[]{:S(2)}, u32[]{:S(2)}) %all-to-all-start.1) | async-done | bytes 393248 | tf_op jit(solution)/shard_map/all_to_all | solution.py:318
  27.2 0.3 pick.2
  27.5 0.0 copy-start.4
  27.5 0.0 copy-done.2
  27.5 0.0 copy-done.3
  27.6 0.7 %copy-done.4 = s32[3,128]{1,0:T(4,128)S(1)} copy-done((s32[3,128]{1,0:T(4,128)S(1)}, s32[3,128]{1,0:T(4,128)}, u32[]{:S(2)}) %copy-start.4) | copy-done | bytes 1560
  28.2 0.6 while.10
  28.9 0.3 broadcast_in_dim.11
  29.2 0.0 copy-start
  29.2 17.3 %all_to_all.16.mine_ref = f32[64,1,2304]{2,1,0:T(1,128)S(1)} all-to-all(f32[64,1,2304]{2,1,0:T(1,128)S(1)} %broadcast_in_dim.11), channel_id=1, replica_groups={{0,2,4,6,8,10,12,14,16,18,20,22,24,26,28,30,32,34,36,38,40,42,44,46,48,..., dimensions={0} | all-to-all | bytes 1179648 | tf_op jit(solution)/shard_map/all_to_all | solution.py:331
  46.5 2.5 %collective-permute-start = (f32[64,1,2304]{2,1,0:T(1,128)S(1)}, f32[64,1,2304]{2,1,0:T(1,128)S(1)}, u32[]{:S(2)}, u32[]{:S(2)}) collective-permute-start(f32[64,1,2304]{2,1,0:T(1,128)S(1)} %all_to_all.16.mine_ref), channel_id=1, source_target_pairs={{0,1},{1,0},{2,3},{3,2},{4,5},{5,4},{6,7},{7,6},{8,9},{9,8},{10,11... | collective-permute-start | bytes 1769480 | tf_op jit(solution)/shard_map/ppermute | solution.py:332
  49.6 0.0 copy-start.1
  49.6 1.0 %collective-permute-done.other_ref = f32[64,1,2304]{2,1,0:T(1,128)S(1)} collective-permute-done((f32[64,1,2304]{2,1,0:T(1,128)S(1)}, f32[64,1,2304]{2,1,0:T(1,128)S(1)}, u32[]{:S(2)}, u32[]{:S(2)}) %collective-permute-start) | collective-permute-done | bytes 589856 | tf_op jit(solution)/shard_map/ppermute | solution.py:332
  50.6 0.0 copy-done
  50.6 0.0 copy-done.1
  50.6 15.2 %window.1 = (f32[384,384]{1,0:T(8,128)}, f32[384]{0:T(512)}) custom-call(f32[1]{0:T(128)S(6)} %copy.14.noise_ref, s32[3,128]{1,0:T(4,128)S(1)} %get-tuple-element.125, f32[1,256]{1,0:T(1,128)S(1)} %bitcast.5, s32[3,384]{1,0:T(4,128)S(1)} %copy-done, f32[64,1,2304]{2,1,0:T(1,128)S(1)} %all_to_all.16.mine_ref, ...), custom_call_target="tpu_custom_call" | custom-call | tf_op jit(solution)/shard_map/window/pallas_call | solution.py:333
  (1 shorter events, 0.0 us)
Async XLA Ops:
  3.6 24.0 %copy-start.2 = (f32[384,512]{1,0:T(8,128)S(1)}, f32[384,512]{1,0:T(8,128)}, u32[]{:S(2)}) copy-start(f32[384,512]{1,0:T(8,128)} %prior_ref.3) | copy-start | bytes 2359300
  3.6 23.6 %all-to-all-start.1 = ((f32[128,1,768]{2,1,0:T(1,128)}), f32[128,1,768]{2,1,0:T(1,128)S(1)}, u32[]{:S(2)}, u32[]{:S(2)}) async-start(f32[128,1,768]{2,1,0:T(1,128)} %get-tuple-element.41), calls=%async_computation.1 | async-start | bytes 786432 | tf_op jit(solution)/shard_map/all_to_all | solution.py:318
  15.1 12.5 %copy-start.3 = (f32[384,256]{1,0:T(8,128)S(1)}, f32[384,256]{1,0:T(8,128)}, u32[]{:S(2)}) copy-start(f32[384,256]{1,0:T(8,128)} %points_ref.3) | copy-start | bytes 1179652
  27.5 0.7 %copy-start.4 = (s32[3,128]{1,0:T(4,128)S(1)}, s32[3,128]{1,0:T(4,128)}, u32[]{:S(2)}) copy-start(s32[3,128]{1,0:T(4,128)} %pivots_ref.3) | copy-start | bytes 4612
  29.2 21.4 %copy-start = (s32[3,384]{1,0:T(4,128)S(1)}, s32[3,384]{1,0:T(4,128)}, u32[]{:S(2)}) copy-start(s32[3,384]{1,0:T(4,128)} %active_ref.1) | copy-start | bytes 13828
  46.5 4.1 %collective-permute-start = (f32[64,1,2304]{2,1,0:T(1,128)S(1)}, f32[64,1,2304]{2,1,0:T(1,128)S(1)}, u32[]{:S(2)}, u32[]{:S(2)}) collective-permute-start(f32[64,1,2304]{2,1,0:T(1,128)S(1)} %all_to_all.16.mine_ref), channel_id=1, source_target_pairs={{0,1},{1,0},{2,3},{3,2},{4,5},{5,4},{6,7},{7,6},{8,9},{9,8},{10,11... | collective-permute-start | bytes 1769480 | tf_op jit(solution)/shard_map/ppermute | solution.py:332
  49.6 1.0 %copy-start.1 = (f32[256]{0:T(256)S(1)}, f32[256]{0:T(256)}, u32[]{:S(2)}) copy-start(f32[256]{0:T(256)} %param.9) | copy-start | bytes 3076

commit v4 on v3

--- a/solution.py
+++ b/solution.py
@@ -46,11 +46,6 @@
     return dot_bf(a[0], b[0], dims) + (dot_bf(a[0], b[1], dims) + dot_bf(a[1], b[0], dims))
 
 
-def six(a, b, dims=NT):
-    small = dot_bf(a[0], b[2], dims) + dot_bf(a[1], b[1], dims) + dot_bf(a[2], b[0], dims)
-    return dot_bf(a[0], b[0], dims) + (dot_bf(a[0], b[1], dims) + dot_bf(a[1], b[0], dims) + small)
-
-
 def column_of(row):
     return jnp.transpose(jnp.broadcast_to(row, (8, 128)))[:, 0:1]
 
@@ -76,12 +71,33 @@
     return jnp.sum(total, axis=0, keepdims=True)
 
 
-def pack_kernel(turn_ref, pivots_ref, points_ref, prior_ref, send_ref, pick_ref, turns_ref):
+def pack_kernel(
+    turn_ref,
+    pivots_ref,
+    points_hbm,
+    prior_hbm,
+    send_ref,
+    pick_ref,
+    turns_ref,
+    kept_ref,
+    points_ref,
+    prior_ref,
+    sems,
+):
+    loads = [
+        pltpu.make_async_copy(source, target, sems.at[i])
+        for i, (source, target) in enumerate(
+            ((points_hbm, points_ref), (prior_hbm, prior_ref))
+        )
+    ]
+    for load in loads:
+        load.start()
     rows = points_ref.shape[0]
     devices = send_ref.shape[0]
     index = lax.axis_index("rows")
     turn = turn_ref[0].astype(F32)
     base = (index * rows).astype(F32)
+    kept_ref[...] = pivots_ref[...]
     columns = pivot_columns(pivots_ref)
     ids = base + lax.broadcasted_iota(jnp.int32, (1, rows), 1).astype(F32)
     place = count_rows([column < ids for column in columns])
@@ -91,12 +107,6 @@
     home = jnp.where((found > 0.5) & (step >= 0.0) & (step < devices), home, -1.0)
     target = lax.broadcasted_iota(jnp.int32, (devices, rows), 0).astype(F32)
     select = (target == home).astype(BF)
-    at = 0
-    for ref in (points_ref, prior_ref):
-        high, mid, low = split3(ref[...])
-        got = dot_bf(select, high, NN) + dot_bf(select, mid, NN) + dot_bf(select, low, NN)
-        send_ref[:, 0, at : at + got.shape[1]] = got
-        at += got.shape[1]
     edges = rows * lax.broadcasted_iota(jnp.int32, (1, devices), 1).astype(F32)
     start = count_rows([column < edges for column in columns])
     stop = count_rows([column < edges + rows for column in columns])
@@ -107,6 +117,13 @@
     pick_ref[...] = (pick & (slot < PIV // devices)).astype(F32)
     longest = jnp.max(stop - start)
     turns_ref[0] = jnp.where(longest > 2 * devices, 3, jnp.where(longest > devices, 2, 1))
+    at = 0
+    for load, ref in ((loads[0], points_ref), (loads[1], prior_ref)):
+        load.wait()
+        high, mid, low = split3(ref[...])
+        got = dot_bf(select, high, NN) + dot_bf(select, mid, NN) + dot_bf(select, low, NN)
+        send_ref[:, 0, at : at + got.shape[1]] = got
+        at += got.shape[1]
 
 
 def pick_kernel(pick_ref, came_ref, out_ref, rows_ref):
@@ -219,9 +236,9 @@
     half, turn, home = lane // HALF, lane % HALF // homes, lane % homes
     held = (2 * home + half + 2 * homes * turn).astype(F32)
     place = (order == held).astype(BF)
-    pp3 = [dot_bf(place, part, NN) for part in split3(g_ref[:, 0:D] * scale)]
-    pp = pp3[0] + pp3[1] + pp3[2]
-    pp3 = [part.astype(BF) for part in pp3]
+    pp2 = [dot_bf(place, part, NN) for part in split2(g_ref[:, 0:D] * scale)]
+    pp = pp2[0] + pp2[1]
+    pp2 = [part.astype(BF) for part in pp2]
     pf2 = [dot_bf(place, part, NN).astype(BF) for part in split2(g_ref[:, D:F])]
     square_col = jnp.sum(pp * pp, axis=1, keepdims=True)
     square_row = jnp.concatenate(
@@ -231,12 +248,18 @@
         lax.broadcasted_iota(jnp.int32, (PIV, PIV), 0)
         == lax.broadcasted_iota(jnp.int32, (PIV, PIV), 1)
     ).astype(F32)
-    gram = jnp.exp(-0.5 * (square_col + square_row - 2.0 * six(pp3, pp3))) + noise * eye
-    k_ref[...] = gram - three(pf2, pf2)
+    for low, high in ((0, 2 * PANEL), (2 * PANEL, PIV)):
+        down = [slice(low, PIV), slice(low, high)]
+        inner = three([part[down[0]] for part in pp2], [part[down[1]] for part in pp2])
+        gram = jnp.exp(-0.5 * (square_col[down[0]] + square_row[:, down[1]] - 2.0 * inner))
+        gram = gram + noise * eye[down[0], down[1]]
+        k_ref[down[0], down[1]] = gram - three(
+            [part[down[0]] for part in pf2], [part[down[1]] for part in pf2]
+        )
     mine = points_ref[...] * scale
     prior = prior_ref[...]
     mine_col = jnp.sum(mine * mine, axis=1, keepdims=True)
-    residual = jnp.exp(-0.5 * (mine_col + square_row - 2.0 * six(split3(mine), pp3)))
+    residual = jnp.exp(-0.5 * (mine_col + square_row - 2.0 * three(split2(mine), pp2)))
     residual = residual - three(split2(prior), pf2)
     ids = base + lax.broadcasted_iota(jnp.int32, (rows, PANEL), 0)
     for panel in range(PANELS):
@@ -283,6 +306,7 @@
 VMEM = pl.BlockSpec(memory_space=pltpu.VMEM)
 SMALL = pltpu.CompilerParams(vmem_limit_bytes=16 * 1024 * 1024)
 ANY = pl.BlockSpec(memory_space=pl.ANY)
+HBM = pl.BlockSpec(memory_space=pltpu.HBM)
 
 
 def local(points, inv_scale, noise, prior, active, pivots):
@@ -294,16 +318,22 @@
     exchange = functools.partial(
         lax.all_to_all, axis_name="rows", split_axis=0, concat_axis=0, tiled=True
     )
-    def routed(turn):
-        send, pick, turns = pl.pallas_call(
+    def routed(turn, pivots):
+        send, pick, turns, kept = pl.pallas_call(
             pack_kernel,
             out_shape=(
                 jax.ShapeDtypeStruct((devices, 1, F), F32),
                 jax.ShapeDtypeStruct((8, devices), F32),
                 jax.ShapeDtypeStruct((1,), jnp.int32),
+                jax.ShapeDtypeStruct((PANELS, PANEL), jnp.int32),
             ),
-            in_specs=[SMEM, VMEM, VMEM, VMEM],
-            out_specs=(VMEM, VMEM, SMEM),
+            in_specs=[SMEM, VMEM, HBM, HBM],
+            out_specs=(VMEM, VMEM, SMEM, VMEM),
+            scratch_shapes=[
+                pltpu.VMEM((rows, D), F32),
+                pltpu.VMEM((rows, R0), F32),
+                pltpu.SemaphoreType.DMA((2,)),
+            ],
             name="pack",
             compiler_params=SMALL,
         )(turn, pivots, points, prior)
@@ -316,16 +346,16 @@
             name="pick",
             compiler_params=SMALL,
         )(pick, exchange(send))
-        return owned, turns[0]
-
-    owned, turns = routed(jnp.zeros((1,), jnp.int32))
+        return owned, turns[0], kept
+
+    owned, turns, pivots = routed(jnp.zeros((1,), jnp.int32), pivots)
 
     def more(state):
         return state[0] < turns
 
     def again(state):
         turn, owned = state
-        return turn + 1, owned + routed(turn[None])[0]
+        return turn + 1, owned + routed(turn[None], pivots)[0]
 
     owned = lax.while_loop(more, again, (jnp.int32(1), owned))[1]
     mine = exchange(jnp.broadcast_to(owned, (homes, *owned.shape[1:])), axis_index_groups=groups)

time: 66.2 us -> 65.2 us (0.985)
  Pallas kernels: 18.4 us -> 17.4 us
    pallas_call x1, Pallas kernels: 15.2 us -> 14.1 us  [local(): pl.pallas_call(window_kernel, out_shape=(jax.ShapeDtypeStruct((rows, PIV)...]
where the time goes in v4:
time: 65.2 us; the launch traced here: 64.9 us
  Pallas kernels  17.4 us (27%)
  blocking collectives  17.3 us (27%)
  starting transfers between devices  14 us (21%)
  waiting for transfers between devices  13.1 us (20%)
  between operations  1.54 us (2%)
  local copies, waits for them, and re-layouts  1.01 us (2%)
    all_to_all x1, blocking collectives, local(): exchange(jnp.broadcast_to(owned, (homes, *owned.shape[1:])), axis_index_g...  17.3 us
    pallas_call x1, Pallas kernels, local(): pl.pallas_call(window_kernel, out_shape=(jax.ShapeDtypeStruct((rows, PIV)...  14.1 us
    all_to_all x1, waiting for transfers between devices, routed(): exchange(send)  12.1 us
    all_to_all x1, starting transfers between devices, routed(): exchange(send)  11.5 us
    pallas_call x1, Pallas kernels, routed(): pl.pallas_call(pack_kernel, out_shape=(jax.ShapeDtypeStruct((devices, 1,...  2.98 us
    ppermute x1, starting transfers between devices, local(): other = lax.ppermute(mine, 'rows', partner)  2.46 us
  transfers between devices with their start and end apart: 2, of which 2 were waited for; matrix products, arithmetic and copies ran while one was open for 0% of the time, Pallas kernels for 0%

profile of v4, /device:TPU:1, one launch (start us, length us, event | category | flops | bytes accessed | tf_op | source)
XLA Modules:
  0.0 64.9 jit_solution(3652380539555152672)
XLA Ops:
  0.6 0.0 copy-start.1
  0.6 0.7 %copy-done.1 = s32[3,128]{1,0:T(4,128)S(1)} copy-done((s32[3,128]{1,0:T(4,128)S(1)}, s32[3,128]{1,0:T(4,128)}, u32[]{:S(2)}) %copy-start.1) | copy-done | bytes 1560
  1.3 3.0 %pack.2 = (f32[128,1,768]{2,1,0:T(1,128)}, f32[8,128]{1,0:T(8,128)S(1)}, s32[1]{0:T(128)}, s32[3,128]{1,0:T(4,128)S(1)}) custom-call(s32[1]{0:T(128)} %constant.1.clone.1.turn_ref, s32[3,128]{1,0:T(4,128)S(1)} %copy-done.1, f32[384,256]{1,0:T(8,128)} %points_ref.1, f32[384,512]{1,0:T(8,128)} %prior_ref.1), custom_call_target="tpu_custom_call" | custom-call | tf_op jit(solution)/shard_map/pack/pallas_call | solution.py:322
  4.3 0.0 copy-start.3
  4.3 11.5 %all-to-all-start.1 = ((f32[128,1,768]{2,1,0:T(1,128)}), f32[128,1,768]{2,1,0:T(1,128)S(1)}, u32[]{:S(2)}, u32[]{:S(2)}) async-start(f32[128,1,768]{2,1,0:T(1,128)} %get-tuple-element.43), calls=%async_computation.1 | async-start | bytes 786432 | tf_op jit(solution)/shard_map/all_to_all | solution.py:348
  15.8 0.0 copy-start.4
  15.8 12.1 %all-to-all-done.1.came_ref = f32[128,1,768]{2,1,0:T(1,128)S(1)} async-done(((f32[128,1,768]{2,1,0:T(1,128)}), f32[128,1,768]{2,1,0:T(1,128)S(1)}, u32[]{:S(2)}, u32[]{:S(2)}) %all-to-all-start.1) | async-done | bytes 393248 | tf_op jit(solution)/shard_map/all_to_all | solution.py:348
  28.0 0.3 pick.2
  28.2 0.0 copy-done.3
  28.2 0.0 copy-done.4
  28.3 0.6 while.10
  28.9 0.3 broadcast_in_dim.11
  29.3 0.0 copy-start
  29.3 17.3 %all_to_all.16.mine_ref = f32[64,1,2304]{2,1,0:T(1,128)S(1)} all-to-all(f32[64,1,2304]{2,1,0:T(1,128)S(1)} %broadcast_in_dim.11), channel_id=1, replica_groups={{0,2,4,6,8,10,12,14,16,18,20,22,24,26,28,30,32,34,36,38,40,42,44,46,48,..., dimensions={0} | all-to-all | bytes 1179648 | tf_op jit(solution)/shard_map/all_to_all | solution.py:361
  46.5 2.5 %collective-permute-start = (f32[64,1,2304]{2,1,0:T(1,128)S(1)}, f32[64,1,2304]{2,1,0:T(1,128)S(1)}, u32[]{:S(2)}, u32[]{:S(2)}) collective-permute-start(f32[64,1,2304]{2,1,0:T(1,128)S(1)} %all_to_all.16.mine_ref), channel_id=1, source_target_pairs={{0,1},{1,0},{2,3},{3,2},{4,5},{5,4},{6,7},{7,6},{8,9},{9,8},{10,11... | collective-permute-start | bytes 1769480 | tf_op jit(solution)/shard_map/ppermute | solution.py:362
  49.6 0.0 copy-start.2
  49.7 1.0 %collective-permute-done.other_ref = f32[64,1,2304]{2,1,0:T(1,128)S(1)} collective-permute-done((f32[64,1,2304]{2,1,0:T(1,128)S(1)}, f32[64,1,2304]{2,1,0:T(1,128)S(1)}, u32[]{:S(2)}, u32[]{:S(2)}) %collective-permute-start) | collective-permute-done | bytes 589856 | tf_op jit(solution)/shard_map/ppermute | solution.py:362
  50.6 0.0 copy-done
  50.6 0.0 copy-done.2
  50.6 14.1 %window.1 = (f32[384,384]{1,0:T(8,128)}, f32[384]{0:T(512)}) custom-call(f32[1]{0:T(128)S(6)} %copy.14.noise_ref, s32[3,128]{1,0:T(4,128)S(1)} %get-tuple-element.127, f32[1,256]{1,0:T(1,128)S(1)} %bitcast.5, s32[3,384]{1,0:T(4,128)S(1)} %copy-done, f32[64,1,2304]{2,1,0:T(1,128)S(1)} %all_to_all.16.mine_ref, ...), custom_call_target="tpu_custom_call" | custom-call | tf_op jit(solution)/shard_map/window/pallas_call | solution.py:363
  (1 shorter events, 0.0 us)
Async XLA Ops:
  0.6 0.7 %copy-start.1 = (s32[3,128]{1,0:T(4,128)S(1)}, s32[3,128]{1,0:T(4,128)}, u32[]{:S(2)}) copy-start(s32[3,128]{1,0:T(4,128)} %pivots_ref.1) | copy-start | bytes 4612
  4.3 23.9 %copy-start.3 = (f32[384,512]{1,0:T(8,128)S(1)}, f32[384,512]{1,0:T(8,128)}, u32[]{:S(2)}) copy-start(f32[384,512]{1,0:T(8,128)} %prior_ref.1) | copy-start | bytes 2359300
  4.3 23.6 %all-to-all-start.1 = ((f32[128,1,768]{2,1,0:T(1,128)}), f32[128,1,768]{2,1,0:T(1,128)S(1)}, u32[]{:S(2)}, u32[]{:S(2)}) async-start(f32[128,1,768]{2,1,0:T(1,128)} %get-tuple-element.43), calls=%async_computation.1 | async-start | bytes 786432 | tf_op jit(solution)/shard_map/all_to_all | solution.py:348
  15.8 12.4 %copy-start.4 = (f32[384,256]{1,0:T(8,128)S(1)}, f32[384,256]{1,0:T(8,128)}, u32[]{:S(2)}) copy-start(f32[384,256]{1,0:T(8,128)} %points_ref.1) | copy-start | bytes 1179652
  29.3 21.4 %copy-start = (s32[3,384]{1,0:T(4,128)S(1)}, s32[3,384]{1,0:T(4,128)}, u32[]{:S(2)}) copy-start(s32[3,384]{1,0:T(4,128)} %active_ref.1) | copy-start | bytes 13828
  46.5 4.1 %collective-permute-start = (f32[64,1,2304]{2,1,0:T(1,128)S(1)}, f32[64,1,2304]{2,1,0:T(1,128)S(1)}, u32[]{:S(2)}, u32[]{:S(2)}) collective-permute-start(f32[64,1,2304]{2,1,0:T(1,128)S(1)} %all_to_all.16.mine_ref), channel_id=1, source_target_pairs={{0,1},{1,0},{2,3},{3,2},{4,5},{5,4},{6,7},{7,6},{8,9},{9,8},{10,11... | collective-permute-start | bytes 1769480 | tf_op jit(solution)/shard_map/ppermute | solution.py:362
  49.6 1.0 %copy-start.2 = (f32[256]{0:T(256)S(1)}, f32[256]{0:T(256)}, u32[]{:S(2)}) copy-start(f32[256]{0:T(256)} %param.9) | copy-start | bytes 3076

commit v5 on v4

--- a/solution.py
+++ b/solution.py
@@ -13,6 +13,7 @@
 PANEL = 128
 PANELS = 3
 PIV = PANEL * PANELS
+FAR = 1e9
 HALF = PIV // 2
 STRIP = 8
 LOOK = 2
@@ -54,21 +55,29 @@
     return [column_of(pivots_ref[p : p + 1, :].astype(F32)) for p in range(PANELS)]
 
 
-def pivot_order(pivots_ref):
-    smaller = []
-    for column in pivot_columns(pivots_ref):
-        ahead = [
-            (pivots_ref[p : p + 1, :].astype(F32) < column).astype(F32) for p in range(PANELS)
-        ]
-        smaller.append(jnp.sum(ahead[0] + ahead[1] + ahead[2], axis=1, keepdims=True))
-    return jnp.concatenate(smaller, axis=0)
-
-
-def count_rows(tests):
-    total = tests[0].astype(F32)
-    for test in tests[1:]:
-        total = total + test.astype(F32)
-    return jnp.sum(total, axis=0, keepdims=True)
+def halves(parts):
+    cut = PANEL // 2
+    return (
+        [parts[0], parts[1][0:cut]],
+        [parts[1][cut:PANEL], parts[2]],
+    )
+
+
+def place_in_half(pivots_ref, half):
+    lane = lax.broadcasted_iota(jnp.int32, (1, PANEL), 1)
+    rows = [pivots_ref[p : p + 1, :].astype(F32) for p in range(PANELS)]
+    mixed = jnp.where((lane < PANEL // 2) == (half == 0), rows[1], FAR)
+    order = []
+    for column in halves(pivot_columns(pivots_ref))[half]:
+        ahead = (rows[2 * half] < column).astype(F32) + (mixed < column).astype(F32)
+        order.append(jnp.sum(ahead, axis=1, keepdims=True))
+    order = jnp.concatenate(order, axis=0)
+    held = lax.broadcasted_iota(jnp.int32, (HALF, HALF), 1).astype(F32)
+    return (order == held).astype(BF)
+
+
+def count_halves(tests):
+    return sum(jnp.sum(test.astype(F32), axis=0, keepdims=True) for test in tests)
 
 
 def pack_kernel(
@@ -98,25 +107,33 @@
     turn = turn_ref[0].astype(F32)
     base = (index * rows).astype(F32)
     kept_ref[...] = pivots_ref[...]
-    columns = pivot_columns(pivots_ref)
     ids = base + lax.broadcasted_iota(jnp.int32, (1, rows), 1).astype(F32)
-    place = count_rows([column < ids for column in columns])
-    found = count_rows([column == ids for column in columns])
-    step = place - place[:, 0:1] - devices * turn
-    home = place - devices * jnp.floor(place * (1.0 / devices))
-    home = jnp.where((found > 0.5) & (step >= 0.0) & (step < devices), home, -1.0)
+    homes = devices // 2
     target = lax.broadcasted_iota(jnp.int32, (devices, rows), 0).astype(F32)
-    select = (target == home).astype(BF)
     edges = rows * lax.broadcasted_iota(jnp.int32, (1, devices), 1).astype(F32)
-    start = count_rows([column < edges for column in columns])
-    stop = count_rows([column < edges + rows for column in columns])
     slot = lax.broadcasted_iota(jnp.int32, (8, devices), 0)
-    wanted = index.astype(F32) + devices * slot.astype(F32)
-    step = wanted - start - devices * turn
-    pick = (wanted >= start) & (wanted < stop) & (step >= 0.0) & (step < devices)
-    pick_ref[...] = (pick & (slot < PIV // devices)).astype(F32)
-    longest = jnp.max(stop - start)
-    turns_ref[0] = jnp.where(longest > 2 * devices, 3, jnp.where(longest > devices, 2, 1))
+    core = lax.rem(index, 2)
+    wanted = (index // 2).astype(F32) + homes * slot.astype(F32)
+    select, pick, longest = None, None, None
+    for half, columns in enumerate(halves(pivot_columns(pivots_ref))):
+        place = count_halves([column < ids for column in columns])
+        found = count_halves([column == ids for column in columns])
+        step = place - place[:, 0:1] - homes * turn
+        home = 2.0 * (place - homes * jnp.floor(place * (1.0 / homes))) + half
+        home = jnp.where((found > 0.5) & (step >= 0.0) & (step < homes), home, -1.0)
+        start = count_halves([column < edges for column in columns])
+        stop = count_halves([column < edges + rows for column in columns])
+        step = wanted - start - homes * turn
+        mine = (wanted >= start) & (wanted < stop) & (step >= 0.0) & (step < homes)
+        mine = mine & (slot < HALF // homes) & (core == half)
+        hit = target == home
+        run = jnp.max(stop - start)
+        select = hit if half == 0 else select | hit
+        pick = mine if half == 0 else pick | mine
+        longest = run if half == 0 else jnp.maximum(longest, run)
+    select = select.astype(BF)
+    pick_ref[...] = pick.astype(F32)
+    turns_ref[0] = jnp.where(longest > 2 * homes, 3, jnp.where(longest > homes, 2, 1))
     at = 0
     for load, ref in ((loads[0], points_ref), (loads[1], prior_ref)):
         load.wait()
@@ -201,17 +218,98 @@
     return jnp.transpose(jnp.broadcast_to(column, (PANEL, PANEL)))[0:1, :]
 
 
+def prepare_kernel(
+    pivots_ref, scale_ref, points_ref, prior_ref, mine_ref, prior2_ref, sums_ref, place_ref
+):
+    mine = points_ref[...] * scale_ref[...]
+    prior = prior_ref[...]
+    for ref, value in ((mine_ref, mine), (prior2_ref, prior)):
+        ref[0], ref[1] = split2(value)
+    for row, value in enumerate((mine, prior)):
+        total = jnp.sum(value * value, axis=1, keepdims=True)
+        for i in range(value.shape[0] // 128):
+            here = slice(i * 128, (i + 1) * 128)
+            sums_ref[row : row + 1, here] = row_of(total[here])
+    for half in range(2):
+        place_ref[half] = place_in_half(pivots_ref, half)
+
+
+def half_of(half, noise, pivots_ref, scale_ref, place_ref, sums_ref, mine_ref, prior_ref, buf_ref, g_ref):
+    homes = buf_ref.shape[0]
+    rows = mine_ref.shape[1]
+    for turn in range(HALF // homes):
+        g_ref[turn * homes : (turn + 1) * homes, :] = buf_ref[:, 0, turn * F : (turn + 1) * F]
+    place = place_ref[half]
+    near = [dot_bf(place, part, NN) for part in split2(g_ref[:, 0:D] * scale_ref[...])]
+    both = near[0] + near[1]
+    near = [part.astype(BF) for part in near]
+    factor_rows = [dot_bf(place, part, NN).astype(BF) for part in split2(g_ref[:, D:F])]
+    square = jnp.sum(both * both, axis=1, keepdims=True)
+    inner = three(near, (mine_ref[0], mine_ref[1]))
+    residual = jnp.exp(-0.5 * (square + sums_ref[0:1, :] - 2.0 * inner))
+    residual = residual - three(factor_rows, (prior_ref[0], prior_ref[1]))
+    first, second = halves(pivot_columns(pivots_ref))
+    wanted = jnp.where(half == 0, jnp.concatenate(first, 0), jnp.concatenate(second, 0))
+    ids = lax.axis_index("rows") * rows + lax.broadcasted_iota(jnp.int32, (1, rows), 1)
+    residual = residual + noise * (wanted == ids.astype(F32)).astype(F32)
+    return near, factor_rows, square, residual
+
+
+def half_kernel(
+    noise_ref,
+    pivots_ref,
+    scale_ref,
+    place_ref,
+    sums_ref,
+    mine_ref,
+    prior_ref,
+    buf_ref,
+    near_ref,
+    rows_ref,
+    square_ref,
+    residual_ref,
+    g_ref,
+):
+    half = lax.rem(lax.axis_index("rows"), 2)
+    near, factor_rows, square, residual = half_of(
+        half,
+        noise_ref[0],
+        pivots_ref,
+        scale_ref,
+        place_ref,
+        sums_ref,
+        mine_ref,
+        prior_ref,
+        buf_ref,
+        g_ref,
+    )
+    for part in range(2):
+        near_ref[part] = near[part]
+        rows_ref[part] = factor_rows[part]
+    square_ref[...] = square
+    residual_ref[...] = residual
+
+
 def window_kernel(
     noise_ref,
     pivots_ref,
     scale_ref,
+    place_ref,
+    sums_ref,
+    mine_ref,
+    prior_ref,
+    buf_ref,
+    own_near_ref,
+    own_rows_ref,
+    own_square_ref,
+    own_residual_ref,
     active_ref,
-    mine_ref,
-    other_ref,
-    points_ref,
-    prior_ref,
     new_hbm,
     diag_ref,
+    near_ref,
+    rows_ref,
+    square_ref,
+    r_ref,
     g_ref,
     k_ref,
     w_ref,
@@ -220,27 +318,33 @@
     x_ref,
     out_sems,
 ):
-    rows = points_ref.shape[0]
-    homes = mine_ref.shape[0]
-    index = lax.axis_index("rows")
-    core = lax.rem(index, 2)
-    base = index * rows
+    rows = mine_ref.shape[1]
     noise = noise_ref[0]
-    scale = scale_ref[...]
-    for ref, half in ((mine_ref, core), (other_ref, 1 - core)):
-        for turn in range(HALF // homes):
-            at = pl.ds(pl.multiple_of(half * HALF, HALF) + turn * homes, homes)
-            g_ref[at, :] = ref[:, 0, turn * F : (turn + 1) * F]
-    order = pivot_order(pivots_ref)
-    lane = lax.broadcasted_iota(jnp.int32, (1, PIV), 1)
-    half, turn, home = lane // HALF, lane % HALF // homes, lane % homes
-    held = (2 * home + half + 2 * homes * turn).astype(F32)
-    place = (order == held).astype(BF)
-    pp2 = [dot_bf(place, part, NN) for part in split2(g_ref[:, 0:D] * scale)]
-    pp = pp2[0] + pp2[1]
-    pp2 = [part.astype(BF) for part in pp2]
-    pf2 = [dot_bf(place, part, NN).astype(BF) for part in split2(g_ref[:, D:F])]
-    square_col = jnp.sum(pp * pp, axis=1, keepdims=True)
+    core = lax.rem(lax.axis_index("rows"), 2)
+    here = pl.ds(pl.multiple_of(core * HALF, HALF), HALF)
+    there = pl.ds(pl.multiple_of((1 - core) * HALF, HALF), HALF)
+    near, factor_rows, square, residual = half_of(
+        1 - core,
+        noise,
+        pivots_ref,
+        scale_ref,
+        place_ref,
+        sums_ref,
+        mine_ref,
+        prior_ref,
+        buf_ref,
+        g_ref,
+    )
+    for part in range(2):
+        near_ref[part, here, :] = own_near_ref[part]
+        near_ref[part, there, :] = near[part]
+        rows_ref[part, here, :] = own_rows_ref[part]
+        rows_ref[part, there, :] = factor_rows[part]
+    square_ref[here, :] = own_square_ref[...]
+    square_ref[there, :] = square
+    r_ref[here, :] = own_residual_ref[...]
+    r_ref[there, :] = residual
+    square_col = square_ref[...]
     square_row = jnp.concatenate(
         [row_of(square_col[i * PANEL : (i + 1) * PANEL]) for i in range(PANELS)], axis=1
     )
@@ -249,25 +353,18 @@
         == lax.broadcasted_iota(jnp.int32, (PIV, PIV), 1)
     ).astype(F32)
     for low, high in ((0, 2 * PANEL), (2 * PANEL, PIV)):
-        down = [slice(low, PIV), slice(low, high)]
-        inner = three([part[down[0]] for part in pp2], [part[down[1]] for part in pp2])
-        gram = jnp.exp(-0.5 * (square_col[down[0]] + square_row[:, down[1]] - 2.0 * inner))
-        gram = gram + noise * eye[down[0], down[1]]
-        k_ref[down[0], down[1]] = gram - three(
-            [part[down[0]] for part in pf2], [part[down[1]] for part in pf2]
+        down, over = slice(low, PIV), slice(low, high)
+        inner = three(
+            (near_ref[0, down, :], near_ref[1, down, :]),
+            (near_ref[0, over, :], near_ref[1, over, :]),
         )
-    mine = points_ref[...] * scale
-    prior = prior_ref[...]
-    mine_col = jnp.sum(mine * mine, axis=1, keepdims=True)
-    residual = jnp.exp(-0.5 * (mine_col + square_row - 2.0 * three(split2(mine), pp2)))
-    residual = residual - three(split2(prior), pf2)
-    ids = base + lax.broadcasted_iota(jnp.int32, (rows, PANEL), 0)
-    for panel in range(PANELS):
-        span = slice(panel * PANEL, (panel + 1) * PANEL)
-        same = (ids == pivots_ref[panel : panel + 1, :]).astype(F32)
-        x_ref[:, span] = residual[:, span] + noise * same
+        gram = jnp.exp(-0.5 * (square_col[down] + square_row[:, over] - 2.0 * inner))
+        k_ref[down, over] = (gram + noise * eye[down, over]) - three(
+            (rows_ref[0, down, :], rows_ref[1, down, :]),
+            (rows_ref[0, over, :], rows_ref[1, over, :]),
+        )
     small_eye = eye[0:PANEL, 0:PANEL]
-    total = jnp.sum(prior * prior, axis=1, keepdims=True)
+    total = sums_ref[1:2, :]
     stores = []
     for panel in range(PANELS):
         span = slice(panel * PANEL, (panel + 1) * PANEL)
@@ -279,25 +376,19 @@
             rest = slice((panel + 1) * PANEL, PIV)
             below = split2(three(split2(k_ref[rest, span]), inverse))
             k_ref[rest, rest] = k_ref[rest, rest] - three(below, below)
-        fresh = three(split2(x_ref[:, span]), inverse)
-        mask = jnp.concatenate(
-            [
-                column_of(active_ref[panel : panel + 1, i * 128 : (i + 1) * 128].astype(F32))
-                for i in range(rows // 128)
-            ],
-            axis=0,
-        )
-        fresh = fresh * mask
-        x_ref[:, span] = fresh
+        fresh = three(inverse, split2(r_ref[span, :]), NN)
+        fresh = fresh * active_ref[panel : panel + 1, :].astype(F32)
+        total = total + jnp.sum(fresh * fresh, axis=0, keepdims=True)
+        x_ref[:, span] = jnp.transpose(fresh)
         store = pltpu.make_async_copy(x_ref.at[:, span], new_hbm.at[:, span], out_sems.at[panel])
         store.start()
         stores.append(store)
-        total = total + jnp.sum(fresh * fresh, axis=1, keepdims=True)
         if panel + 1 < PANELS:
-            x_ref[:, rest] = x_ref[:, rest] - three(split2(fresh), below)
+            r_ref[rest, :] = r_ref[rest, :] - three(below, split2(fresh), NN)
     diag = (1.0 + noise) - total
     for i in range(rows // 128):
-        diag_ref[i * 128 : (i + 1) * 128] = row_of(diag[i * 128 : (i + 1) * 128])[0]
+        span = slice(i * 128, (i + 1) * 128)
+        diag_ref[span] = diag[0, span]
     for store in stores:
         store.wait()
 
@@ -350,6 +441,24 @@
 
     owned, turns, pivots = routed(jnp.zeros((1,), jnp.int32), pivots)
 
+    scale = inv_scale.reshape(1, D)
+    mine2, prior2, sums, place = pl.pallas_call(
+        prepare_kernel,
+        out_shape=(
+            jax.ShapeDtypeStruct((2, rows, D), BF),
+            jax.ShapeDtypeStruct((2, rows, R0), BF),
+            jax.ShapeDtypeStruct((2, rows), F32),
+            jax.ShapeDtypeStruct((2, HALF, HALF), BF),
+        ),
+        in_specs=[VMEM] * 4,
+        out_specs=(VMEM,) * 4,
+        name="prepare",
+        compiler_params=SMALL,
+    )(pivots, scale, points, prior)
+    owned, mine2, prior2, sums, place = lax.optimization_barrier(
+        (owned, mine2, prior2, sums, place)
+    )
+
     def more(state):
         return state[0] < turns
 
@@ -360,16 +469,35 @@
     owned = lax.while_loop(more, again, (jnp.int32(1), owned))[1]
     mine = exchange(jnp.broadcast_to(owned, (homes, *owned.shape[1:])), axis_index_groups=groups)
     other = lax.ppermute(mine, "rows", partner)
+    common = (noise, pivots, scale, place, sums, mine2, prior2)
+    own = pl.pallas_call(
+        half_kernel,
+        out_shape=(
+            jax.ShapeDtypeStruct((2, HALF, D), BF),
+            jax.ShapeDtypeStruct((2, HALF, R0), BF),
+            jax.ShapeDtypeStruct((HALF, 1), F32),
+            jax.ShapeDtypeStruct((HALF, rows), F32),
+        ),
+        in_specs=[SMEM] + [VMEM] * 7,
+        out_specs=(VMEM,) * 4,
+        scratch_shapes=[pltpu.VMEM((HALF, F), F32)],
+        name="half",
+        compiler_params=SMALL,
+    )(*common, mine)
     return pl.pallas_call(
         window_kernel,
         out_shape=(
             jax.ShapeDtypeStruct((rows, PIV), F32),
             jax.ShapeDtypeStruct((rows,), F32),
         ),
-        in_specs=[SMEM] + [VMEM] * 7,
+        in_specs=[SMEM] + [VMEM] * 12,
         out_specs=(ANY, VMEM),
         scratch_shapes=[
-            pltpu.VMEM((PIV, F), F32),
+            pltpu.VMEM((2, PIV, D), BF),
+            pltpu.VMEM((2, PIV, R0), BF),
+            pltpu.VMEM((PIV, 1), F32),
+            pltpu.VMEM((PIV, rows), F32),
+            pltpu.VMEM((HALF, F), F32),
             pltpu.VMEM((PIV, PIV), F32),
             pltpu.VMEM((PANEL, 2 * PANEL), F32),
             pltpu.VMEM((PANEL, 2 * PANEL), F32),
@@ -379,7 +507,7 @@
         ],
         name="window",
         compiler_params=SMALL,
-    )(noise, pivots, inv_scale.reshape(1, D), active, mine, other, points, prior)
+    )(*common, other, *own, active)
 
 
 def solution(mesh):

time: 65.2 us -> 64.1 us (0.983)
  waiting for transfers between devices: 13.1 us -> 10.2 us
  local copies, waits for them, and re-layouts: 1.01 us -> 2.32 us
    pallas_call x0 -> x2, Pallas kernels: none -> 2.23 us  [the longest x1 1.25 us: local(): pl.pallas_call(prepare_kernel, out_shape=(jax.ShapeDtypeStruct((2, rows,...]
    all_to_all x1, waiting for transfers between devices: 12.1 us -> 10.2 us  [routed(): exchange(send)]
    pallas_call x1, Pallas kernels: 14.1 us -> 12.4 us  [local(): pl.pallas_call(window_kernel, out_shape=(jax.ShapeDtypeStruct((rows, PIV)...]
    unnamed x10, local copies, waits for them, and re-layouts: 0.7 us -> 2.02 us
    ppermute x1, waiting for transfers between devices: 0.97 us -> 0.01 us  [local(): other = lax.ppermute(mine, 'rows', partner)]
  transfers between devices with their start and end apart: 2 -> 2, of which waited for: 2 -> 1; matrix products, arithmetic and copies ran while one was open for 0% -> 0% of each run, Pallas kernels for 0% -> 3%
where the time goes in v5:
time: 64.1 us; the launch traced here: 63.8 us
  Pallas kernels  17.8 us (28%)
  blocking collectives  17.3 us (27%)
  starting transfers between devices  14 us (22%)
  waiting for transfers between devices  10.2 us (16%)
  local copies, waits for them, and re-layouts  2.32 us (4%)
  between operations  1.56 us (2%)
  loops' own time  0.65 us (1%)
    all_to_all x1, blocking collectives, local(): exchange(jnp.broadcast_to(owned, (homes, *owned.shape[1:])), axis_index_g...  17.3 us
    pallas_call x1, Pallas kernels, local(): pl.pallas_call(window_kernel, out_shape=(jax.ShapeDtypeStruct((rows, PIV)...  12.4 us
    all_to_all x1, starting transfers between devices, routed(): exchange(send)  11.5 us
    all_to_all x1, waiting for transfers between devices, routed(): exchange(send)  10.2 us
    pallas_call x1, Pallas kernels, routed(): pl.pallas_call(pack_kernel, out_shape=(jax.ShapeDtypeStruct((devices, 1,...  2.93 us
    ppermute x1, starting transfers between devices, local(): other = lax.ppermute(mine, 'rows', partner)  2.46 us
    unnamed x10, local copies, waits for them, and re-layouts  2.02 us
  transfers between devices with their start and end apart: 2, of which 1 were waited for; matrix products, arithmetic and copies ran while one was open for 0% of the time, Pallas kernels for 3%

profile of v5, /device:TPU:1, one launch (start us, length us, event | category | flops | bytes accessed | tf_op | source)
XLA Modules:
  0.0 63.8 jit_solution(14896604980290698940)
XLA Ops:
  0.6 0.0 copy-start.2
  0.6 0.7 %copy-done.2 = s32[3,128]{1,0:T(4,128)S(1)} copy-done((s32[3,128]{1,0:T(4,128)S(1)}, s32[3,128]{1,0:T(4,128)}, u32[]{:S(2)}) %copy-start.2) | copy-done | bytes 1560
  1.3 0.0 copy-start.3
  1.3 2.9 %pack.2 = (f32[128,1,768]{2,1,0:T(1,128)}, f32[8,128]{1,0:T(8,128)S(1)}, s32[1]{0:T(128)}, s32[3,128]{1,0:T(4,128)S(1)}) custom-call(s32[1]{0:T(128)} %constant.1.clone.1.turn_ref, s32[3,128]{1,0:T(4,128)S(1)} %copy-done.2, f32[384,256]{1,0:T(8,128)} %points_ref.1, f32[384,512]{1,0:T(8,128)} %prior_ref.1), custom_call_target="tpu_custom_call" | custom-call | tf_op jit(solution)/shard_map/pack/pallas_call | solution.py:413
  4.3 0.0 copy-start.4
  4.3 11.5 %all-to-all-start.1 = ((f32[128,1,768]{2,1,0:T(1,128)}), f32[128,1,768]{2,1,0:T(1,128)S(1)}, u32[]{:S(2)}, u32[]{:S(2)}) async-start(f32[128,1,768]{2,1,0:T(1,128)} %get-tuple-element.56), calls=%async_computation.1 | async-start | bytes 786432 | tf_op jit(solution)/shard_map/all_to_all | solution.py:439
  15.8 0.0 copy-start
  15.8 0.0 copy-done.3
  15.8 0.0 copy-done.4
  15.8 0.7 %copy-done = f32[256]{0:T(256)S(1)} copy-done((f32[256]{0:T(256)S(1)}, f32[256]{0:T(256)}, u32[]{:S(2)}) %copy-start) | copy-done | bytes 1048
  16.4 1.2 %prepare.1 = (bf16[2,384,256]{2,1,0:T(8,128)(2,1)S(1)}, bf16[2,384,512]{2,1,0:T(8,128)(2,1)S(1)}, f32[2,384]{1,0:T(2,128)S(1)}, bf16[2,192,192]{2,1,0:T(8,128)(2,1)S(1)}) custom-call(s32[3,128]{1,0:T(4,128)S(1)} %get-tuple-element.129.pivots_ref, f32[1,256]{1,0:T(1,128)S(1)} %bitcast.5, f32[384,256]{1,0:T(8,128)S(1)} %copy-done.4, f32[384,512]{1,0:T(8,128)S(1)} %copy-done.3), custom_call_target="tpu_custom_call" | custom-call | tf_op jit(solution)/shard_map/prepare/pallas_call | solution.py:445
  17.7 10.2 %all-to-all-done.1.came_ref = f32[128,1,768]{2,1,0:T(1,128)S(1)} async-done(((f32[128,1,768]{2,1,0:T(1,128)}), f32[128,1,768]{2,1,0:T(1,128)S(1)}, u32[]{:S(2)}, u32[]{:S(2)}) %all-to-all-start.1) | async-done | bytes 393248 | tf_op jit(solution)/shard_map/all_to_all | solution.py:439
  27.9 0.3 pick.2
  28.2 0.7 %while.10 = (s32[]{:T(128)}, f32[1,1,2304]{2,1,0:T(1,128)S(1)}, s32[]{:T(128)}, s32[3,128]{1,0:T(4,128)S(1)}, f32[384,256]{1,0:T(8,128)S(1)}, /*index=5*/f32[384,512]{1,0:T(8,128)S(1)}, s32[]{:T(128)}) while((s32[]{:T(128)}, f32[1,1,2304]{2,1,0:T(1,128)S(1)}, s32[]{:T(128)}, s32[3,128]{1,0:T(4,128)S(1)}, f32[384,256]{1,0:T(8,128)S(1)}, ...), condition=%wide.region_1.0_spmd, body=%wide.region_0.0_spmd.sunk | while | flops 2306 | bytes 1207405 | solution.py:469
  28.9 0.3 broadcast_in_dim.11
  29.2 17.3 %all_to_all.16.buf_ref = f32[64,1,2304]{2,1,0:T(1,128)S(1)} all-to-all(f32[64,1,2304]{2,1,0:T(1,128)S(1)} %broadcast_in_dim.11), channel_id=1, replica_groups={{0,2,4,6,8,10,12,14,16,18,20,22,24,26,28,30,32,34,36,38,40,42,44,46,48,..., dimensions={0} | all-to-all | bytes 1179648 | tf_op jit(solution)/shard_map/all_to_all | solution.py:470
  46.5 2.5 %collective-permute-start = (f32[64,1,2304]{2,1,0:T(1,128)S(1)}, f32[64,1,2304]{2,1,0:T(1,128)S(1)}, u32[]{:S(2)}, u32[]{:S(2)}) collective-permute-start(f32[64,1,2304]{2,1,0:T(1,128)S(1)} %all_to_all.16.buf_ref), channel_id=1, source_target_pairs={{0,1},{1,0},{2,3},{3,2},{4,5},{5,4},{6,7},{7,6},{8,9},{9,8},{10,11... | collective-permute-start | bytes 1769480 | tf_op jit(solution)/shard_map/ppermute | solution.py:471
  49.6 1.0 %half.1 = (bf16[2,192,256]{2,1,0:T(8,128)(2,1)S(1)}, bf16[2,192,512]{2,1,0:T(8,128)(2,1)S(1)}, f32[192,1]{1,0:T(8,128)S(1)}, f32[192,384]{1,0:T(8,128)S(1)}) custom-call(f32[1]{0:T(128)S(6)} %copy.14.noise_ref, s32[3,128]{1,0:T(4,128)S(1)} %get-tuple-element.151, f32[1,256]{1,0:T(1,128)S(1)} %bitcast.6, ...), custom_call_target="tpu_custom_call" | custom-call | tf_op jit(solution)/shard_map/half/pallas_call | solution.py:473
  50.6 0.0 copy-start.1
  50.6 0.0 collective-permute-done.buf_ref
  50.6 0.7 %copy-done.1 = s32[3,384]{1,0:T(4,128)S(1)} copy-done((s32[3,384]{1,0:T(4,128)S(1)}, s32[3,384]{1,0:T(4,128)}, u32[]{:S(2)}) %copy-start.1) | copy-done | bytes 4632
  51.3 12.4 %window.1 = (f32[384,384]{1,0:T(8,128)}, f32[384]{0:T(512)}) custom-call(f32[1]{0:T(128)S(6)} %copy.14.noise_ref, s32[3,128]{1,0:T(4,128)S(1)} %get-tuple-element.151, f32[1,256]{1,0:T(1,128)S(1)} %bitcast.7, bf16[2,192,192]{2,1,0:T(8,128)(2,1)S(1)} %get-tuple-element.61.place_ref, f32[2,384]{1,0:T(2,128)S(1)} %get-tuple-element.62.sums_ref, ...), custom_call_target="tpu_custom_call" | custom-call | tf_op jit(solution)/shard_map/window/pallas_call | solution.py:487
  (1 shorter events, 0.0 us)
Async XLA Ops:
  0.6 0.7 %copy-start.2 = (s32[3,128]{1,0:T(4,128)S(1)}, s32[3,128]{1,0:T(4,128)}, u32[]{:S(2)}) copy-start(s32[3,128]{1,0:T(4,128)} %pivots_ref.1) | copy-start | bytes 4612
  1.3 14.5 %copy-start.3 = (f32[384,512]{1,0:T(8,128)S(1)}, f32[384,512]{1,0:T(8,128)}, u32[]{:S(2)}) copy-start(f32[384,512]{1,0:T(8,128)} %prior_ref.1) | copy-start | bytes 2359300
  4.3 11.5 %copy-start.4 = (f32[384,256]{1,0:T(8,128)S(1)}, f32[384,256]{1,0:T(8,128)}, u32[]{:S(2)}) copy-start(f32[384,256]{1,0:T(8,128)} %points_ref.1) | copy-start | bytes 1179652
  4.3 23.6 %all-to-all-start.1 = ((f32[128,1,768]{2,1,0:T(1,128)}), f32[128,1,768]{2,1,0:T(1,128)S(1)}, u32[]{:S(2)}, u32[]{:S(2)}) async-start(f32[128,1,768]{2,1,0:T(1,128)} %get-tuple-element.56), calls=%async_computation.1 | async-start | bytes 786432 | tf_op jit(solution)/shard_map/all_to_all | solution.py:439
  15.8 0.7 %copy-start = (f32[256]{0:T(256)S(1)}, f32[256]{0:T(256)}, u32[]{:S(2)}) copy-start(f32[256]{0:T(256)} %param.9) | copy-start | bytes 3076
  46.5 4.1 %collective-permute-start = (f32[64,1,2304]{2,1,0:T(1,128)S(1)}, f32[64,1,2304]{2,1,0:T(1,128)S(1)}, u32[]{:S(2)}, u32[]{:S(2)}) collective-permute-start(f32[64,1,2304]{2,1,0:T(1,128)S(1)} %all_to_all.16.buf_ref), channel_id=1, source_target_pairs={{0,1},{1,0},{2,3},{3,2},{4,5},{5,4},{6,7},{7,6},{8,9},{9,8},{10,11... | collective-permute-start | bytes 1769480 | tf_op jit(solution)/shard_map/ppermute | solution.py:471
  50.6 0.7 %copy-start.1 = (s32[3,384]{1,0:T(4,128)S(1)}, s32[3,384]{1,0:T(4,128)}, u32[]{:S(2)}) copy-start(s32[3,384]{1,0:T(4,128)} %active_ref.1) | copy-start | bytes 13828

commit v6 on v5

--- a/solution.py
+++ b/solution.py
@@ -82,21 +82,23 @@
 
 def pack_kernel(
     turn_ref,
-    pivots_ref,
+    pivots_hbm,
     points_hbm,
     prior_hbm,
-    send_ref,
+    send_hbm,
     pick_ref,
     turns_ref,
-    kept_ref,
+    pivots_ref,
     points_ref,
     prior_ref,
+    send_ref,
     sems,
+    out_sems,
 ):
     loads = [
         pltpu.make_async_copy(source, target, sems.at[i])
         for i, (source, target) in enumerate(
-            ((points_hbm, points_ref), (prior_hbm, prior_ref))
+            ((pivots_hbm, pivots_ref), (points_hbm, points_ref), (prior_hbm, prior_ref))
         )
     ]
     for load in loads:
@@ -106,7 +108,7 @@
     index = lax.axis_index("rows")
     turn = turn_ref[0].astype(F32)
     base = (index * rows).astype(F32)
-    kept_ref[...] = pivots_ref[...]
+    loads[0].wait()
     ids = base + lax.broadcasted_iota(jnp.int32, (1, rows), 1).astype(F32)
     homes = devices // 2
     target = lax.broadcasted_iota(jnp.int32, (devices, rows), 0).astype(F32)
@@ -135,12 +137,22 @@
     pick_ref[...] = pick.astype(F32)
     turns_ref[0] = jnp.where(longest > 2 * homes, 3, jnp.where(longest > homes, 2, 1))
     at = 0
-    for load, ref in ((loads[0], points_ref), (loads[1], prior_ref)):
+    stores = []
+    for load, ref in ((loads[1], points_ref), (loads[2], prior_ref)):
         load.wait()
         high, mid, low = split3(ref[...])
         got = dot_bf(select, high, NN) + dot_bf(select, mid, NN) + dot_bf(select, low, NN)
-        send_ref[:, 0, at : at + got.shape[1]] = got
+        span = slice(at, at + got.shape[1])
+        send_ref[:, 0, span] = got
         at += got.shape[1]
+        stores.append(
+            pltpu.make_async_copy(
+                send_ref.at[:, :, span], send_hbm.at[:, :, span], out_sems.at[len(stores)]
+            )
+        )
+        stores[-1].start()
+    for store in stores:
+        store.wait()
 
 
 def pick_kernel(pick_ref, came_ref, out_ref, rows_ref):
@@ -219,8 +231,18 @@
 
 
 def prepare_kernel(
-    pivots_ref, scale_ref, points_ref, prior_ref, mine_ref, prior2_ref, sums_ref, place_ref
+    pivots_ref,
+    scale_ref,
+    points_ref,
+    prior_ref,
+    active_ref,
+    mine_ref,
+    prior2_ref,
+    sums_ref,
+    place_ref,
+    mask_ref,
 ):
+    mask_ref[...] = active_ref[...].astype(F32)
     mine = points_ref[...] * scale_ref[...]
     prior = prior_ref[...]
     for ref, value in ((mine_ref, mine), (prior2_ref, prior)):
@@ -303,7 +325,7 @@
     own_rows_ref,
     own_square_ref,
     own_residual_ref,
-    active_ref,
+    mask_ref,
     new_hbm,
     diag_ref,
     near_ref,
@@ -377,7 +399,7 @@
             below = split2(three(split2(k_ref[rest, span]), inverse))
             k_ref[rest, rest] = k_ref[rest, rest] - three(below, below)
         fresh = three(inverse, split2(r_ref[span, :]), NN)
-        fresh = fresh * active_ref[panel : panel + 1, :].astype(F32)
+        fresh = fresh * mask_ref[panel : panel + 1, :]
         total = total + jnp.sum(fresh * fresh, axis=0, keepdims=True)
         x_ref[:, span] = jnp.transpose(fresh)
         store = pltpu.make_async_copy(x_ref.at[:, span], new_hbm.at[:, span], out_sems.at[panel])
@@ -418,11 +440,13 @@
                 jax.ShapeDtypeStruct((1,), jnp.int32),
                 jax.ShapeDtypeStruct((PANELS, PANEL), jnp.int32),
             ),
-            in_specs=[SMEM, VMEM, HBM, HBM],
-            out_specs=(VMEM, VMEM, SMEM, VMEM),
+            in_specs=[SMEM, HBM, HBM, HBM],
+            out_specs=(HBM, VMEM, SMEM, VMEM),
             scratch_shapes=[
                 pltpu.VMEM((rows, D), F32),
                 pltpu.VMEM((rows, R0), F32),
+                pltpu.VMEM((devices, 1, F), F32),
+                pltpu.SemaphoreType.DMA((3,)),
                 pltpu.SemaphoreType.DMA((2,)),
             ],
             name="pack",
@@ -439,24 +463,27 @@
         )(pick, exchange(send))
         return owned, turns[0], kept
 
-    owned, turns, pivots = routed(jnp.zeros((1,), jnp.int32), pivots)
+    owned, turns, pivots = routed(
+        jnp.zeros((1,), jnp.int32), pltpu.with_memory_space_constraint(pivots, pltpu.HBM)
+    )
 
     scale = inv_scale.reshape(1, D)
-    mine2, prior2, sums, place = pl.pallas_call(
+    mine2, prior2, sums, place, mask = pl.pallas_call(
         prepare_kernel,
         out_shape=(
             jax.ShapeDtypeStruct((2, rows, D), BF),
             jax.ShapeDtypeStruct((2, rows, R0), BF),
             jax.ShapeDtypeStruct((2, rows), F32),
             jax.ShapeDtypeStruct((2, HALF, HALF), BF),
+            jax.ShapeDtypeStruct((PANELS, rows), F32),
         ),
-        in_specs=[VMEM] * 4,
-        out_specs=(VMEM,) * 4,
+        in_specs=[VMEM] * 5,
+        out_specs=(VMEM,) * 5,
         name="prepare",
         compiler_params=SMALL,
-    )(pivots, scale, points, prior)
-    owned, mine2, prior2, sums, place = lax.optimization_barrier(
-        (owned, mine2, prior2, sums, place)
+    )(pivots, scale, points, prior, active)
+    owned, mine2, prior2, sums, place, mask = lax.optimization_barrier(
+        (owned, mine2, prior2, sums, place, mask)
     )
 
     def more(state):
@@ -507,7 +534,7 @@
         ],
         name="window",
         compiler_params=SMALL,
-    )(*common, other, *own, active)
+    )(*common, other, *own, mask)
 
 
 def solution(mesh):

time: 64.1 us -> 63.1 us (0.984)
  local copies, waits for them, and re-layouts: 2.32 us -> 0.97 us
    unnamed x10 -> x8, local copies, waits for them, and re-layouts: 2.02 us -> 0.66 us
  transfers between devices with their start and end apart: 2 -> 2, of which waited for: 1 -> 1; matrix products, arithmetic and copies ran while one was open for 0% -> 0% of each run, Pallas kernels for 3% -> 4%
where the time goes in v6:
time: 63.1 us; the launch traced here: 62.8 us
  Pallas kernels  18.2 us (29%)
  blocking collectives  17.3 us (27%)
  starting transfers between devices  14 us (22%)
  waiting for transfers between devices  10.2 us (16%)
  between operations  1.57 us (2%)
  local copies, waits for them, and re-layouts  0.97 us (2%)
  loops' own time  0.64 us (1%)
    all_to_all x1, blocking collectives, local(): exchange(jnp.broadcast_to(owned, (homes, *owned.shape[1:])), axis_index_g...  17.3 us
    pallas_call x1, Pallas kernels, local(): pl.pallas_call(window_kernel, out_shape=(jax.ShapeDtypeStruct((rows, PIV)...  12.4 us
    all_to_all x1, starting transfers between devices, routed(): exchange(send)  11.5 us
    all_to_all x1, waiting for transfers between devices, routed(): exchange(send)  10.2 us
    pallas_call x1, Pallas kernels, routed(): pl.pallas_call(pack_kernel, out_shape=(jax.ShapeDtypeStruct((devices, 1,...  3.3 us
    ppermute x1, starting transfers between devices, local(): other = lax.ppermute(mine, 'rows', partner)  2.46 us
  transfers between devices with their start and end apart: 2, of which 1 were waited for; matrix products, arithmetic and copies ran while one was open for 0% of the time, Pallas kernels for 4%

profile of v6, /device:TPU:1, one launch (start us, length us, event | category | flops | bytes accessed | tf_op | source)
XLA Modules:
  0.0 62.8 jit_solution(17663819358002409151)
XLA Ops:
  0.6 0.0 copy-start.2
  0.6 3.3 %pack.2 = (f32[128,1,768]{2,1,0:T(1,128)}, f32[8,128]{1,0:T(8,128)S(1)}, s32[1]{0:T(128)}, s32[3,128]{1,0:T(4,128)S(1)}) custom-call(s32[1]{0:T(128)} %constant.1.clone.1.turn_ref, s32[3,128]{1,0:T(4,128)} %pivots_hbm.1, f32[384,256]{1,0:T(8,128)} %points_ref.1, f32[384,512]{1,0:T(8,128)} %prior_ref.1), custom_call_target="tpu_custom_call" | custom-call | tf_op jit(solution)/shard_map/pack/pallas_call | solution.py:435
  3.9 0.0 copy-start.1
  4.0 0.0 copy-start.3
  4.0 11.5 %all-to-all-start.1 = ((f32[128,1,768]{2,1,0:T(1,128)}), f32[128,1,768]{2,1,0:T(1,128)S(1)}, u32[]{:S(2)}, u32[]{:S(2)}) async-start(f32[128,1,768]{2,1,0:T(1,128)} %get-tuple-element.58), calls=%async_computation.1 | async-start | bytes 786432 | tf_op jit(solution)/shard_map/all_to_all | solution.py:463
  15.5 0.0 copy-start
  15.5 0.0 copy-done.2
  15.5 0.0 copy-done.1
  15.5 0.0 copy-done.3
  15.5 0.6 %copy-done = f32[256]{0:T(256)S(1)} copy-done((f32[256]{0:T(256)S(1)}, f32[256]{0:T(256)}, u32[]{:S(2)}) %copy-start) | copy-done | bytes 1048
  16.1 1.2 %prepare.1 = (bf16[2,384,256]{2,1,0:T(8,128)(2,1)S(1)}, bf16[2,384,512]{2,1,0:T(8,128)(2,1)S(1)}, f32[2,384]{1,0:T(2,128)S(1)}, bf16[2,192,192]{2,1,0:T(8,128)(2,1)S(1)}, f32[3,384]{1,0:T(4,128)S(1)}) custom-call(s32[3,128]{1,0:T(4,128)S(1)} %get-tuple-element.133.pivots_ref, f32[1,256]{1,0:T(1,128)S(1)} %bitcast.5, f32[384,256]{1,0:T(8,128)S(1)} %copy-done.3, ...), custom_call_target="tpu_custom_call" | custom-call | tf_op jit(solution)/shard_map/prepare/pallas_call | solution.py:471
  17.4 10.2 %all-to-all-done.1.came_ref = f32[128,1,768]{2,1,0:T(1,128)S(1)} async-done(((f32[128,1,768]{2,1,0:T(1,128)}), f32[128,1,768]{2,1,0:T(1,128)S(1)}, u32[]{:S(2)}, u32[]{:S(2)}) %all-to-all-start.1) | async-done | bytes 393248 | tf_op jit(solution)/shard_map/all_to_all | solution.py:463
  27.6 0.3 pick.2
  27.9 0.6 %while.10 = (s32[]{:T(128)}, f32[1,1,2304]{2,1,0:T(1,128)S(1)}, s32[]{:T(128)}, s32[3,128]{1,0:T(4,128)S(1)}, f32[384,256]{1,0:T(8,128)S(1)}, /*index=5*/f32[384,512]{1,0:T(8,128)S(1)}, s32[]{:T(128)}) while((s32[]{:T(128)}, f32[1,1,2304]{2,1,0:T(1,128)S(1)}, s32[]{:T(128)}, s32[3,128]{1,0:T(4,128)S(1)}, f32[384,256]{1,0:T(8,128)S(1)}, ...), condition=%wide.region_1.0_spmd, body=%wide.region_0.0_spmd.sunk | while | flops 2306 | bytes 1207405 | solution.py:496
  28.6 0.3 broadcast_in_dim.11
  28.9 17.3 %all_to_all.16.buf_ref = f32[64,1,2304]{2,1,0:T(1,128)S(1)} all-to-all(f32[64,1,2304]{2,1,0:T(1,128)S(1)} %broadcast_in_dim.11), channel_id=1, replica_groups={{0,2,4,6,8,10,12,14,16,18,20,22,24,26,28,30,32,34,36,38,40,42,44,46,48,..., dimensions={0} | all-to-all | bytes 1179648 | tf_op jit(solution)/shard_map/all_to_all | solution.py:497
  46.2 2.5 %collective-permute-start = (f32[64,1,2304]{2,1,0:T(1,128)S(1)}, f32[64,1,2304]{2,1,0:T(1,128)S(1)}, u32[]{:S(2)}, u32[]{:S(2)}) collective-permute-start(f32[64,1,2304]{2,1,0:T(1,128)S(1)} %all_to_all.16.buf_ref), channel_id=1, source_target_pairs={{0,1},{1,0},{2,3},{3,2},{4,5},{5,4},{6,7},{7,6},{8,9},{9,8},{10,11... | collective-permute-start | bytes 1769480 | tf_op jit(solution)/shard_map/ppermute | solution.py:498
  49.3 1.0 %half.1 = (bf16[2,192,256]{2,1,0:T(8,128)(2,1)S(1)}, bf16[2,192,512]{2,1,0:T(8,128)(2,1)S(1)}, f32[192,1]{1,0:T(8,128)S(1)}, f32[192,384]{1,0:T(8,128)S(1)}) custom-call(f32[1]{0:T(128)S(6)} %copy.14.noise_ref, s32[3,128]{1,0:T(4,128)S(1)} %get-tuple-element.155, f32[1,256]{1,0:T(1,128)S(1)} %bitcast.6, ...), custom_call_target="tpu_custom_call" | custom-call | tf_op jit(solution)/shard_map/half/pallas_call | solution.py:500
  50.3 0.0 collective-permute-done.buf_ref
  50.3 12.4 %window.1 = (f32[384,384]{1,0:T(8,128)}, f32[384]{0:T(512)}) custom-call(f32[1]{0:T(128)S(6)} %copy.14.noise_ref, s32[3,128]{1,0:T(4,128)S(1)} %get-tuple-element.155, f32[1,256]{1,0:T(1,128)S(1)} %bitcast.7, bf16[2,192,192]{2,1,0:T(8,128)(2,1)S(1)} %get-tuple-element.64.place_ref, f32[2,384]{1,0:T(2,128)S(1)} %get-tuple-element.65.sums_ref, ...), custom_call_target="tpu_custom_call" | custom-call | tf_op jit(solution)/shard_map/window/pallas_call | solution.py:514
  (1 shorter events, 0.0 us)
Async XLA Ops:
  0.6 14.9 %copy-start.2 = (f32[384,512]{1,0:T(8,128)S(1)}, f32[384,512]{1,0:T(8,128)}, u32[]{:S(2)}) copy-start(f32[384,512]{1,0:T(8,128)} %prior_ref.1) | copy-start | bytes 2359300
  3.9 11.5 %copy-start.1 = (s32[3,384]{1,0:T(4,128)S(1)}, s32[3,384]{1,0:T(4,128)}, u32[]{:S(2)}) copy-start(s32[3,384]{1,0:T(4,128)} %active_ref.1) | copy-start | bytes 13828
  4.0 11.5 %copy-start.3 = (f32[384,256]{1,0:T(8,128)S(1)}, f32[384,256]{1,0:T(8,128)}, u32[]{:S(2)}) copy-start(f32[384,256]{1,0:T(8,128)} %points_ref.1) | copy-start | bytes 1179652
  4.0 23.6 %all-to-all-start.1 = ((f32[128,1,768]{2,1,0:T(1,128)}), f32[128,1,768]{2,1,0:T(1,128)S(1)}, u32[]{:S(2)}, u32[]{:S(2)}) async-start(f32[128,1,768]{2,1,0:T(1,128)} %get-tuple-element.58), calls=%async_computation.1 | async-start | bytes 786432 | tf_op jit(solution)/shard_map/all_to_all | solution.py:463
  15.5 0.7 %copy-start = (f32[256]{0:T(256)S(1)}, f32[256]{0:T(256)}, u32[]{:S(2)}) copy-start(f32[256]{0:T(256)} %param.9) | copy-start | bytes 3076
  46.2 4.1 %collective-permute-start = (f32[64,1,2304]{2,1,0:T(1,128)S(1)}, f32[64,1,2304]{2,1,0:T(1,128)S(1)}, u32[]{:S(2)}, u32[]{:S(2)}) collective-permute-start(f32[64,1,2304]{2,1,0:T(1,128)S(1)} %all_to_all.16.buf_ref), channel_id=1, source_target_pairs={{0,1},{1,0},{2,3},{3,2},{4,5},{5,4},{6,7},{7,6},{8,9},{9,8},{10,11... | collective-permute-start | bytes 1769480 | tf_op jit(solution)/shard_map/ppermute | solution.py:498

commit v7 on v6

--- a/solution.py
+++ b/solution.py
@@ -205,7 +205,7 @@
             inv_ref[first + j : first + j + 1, :] = row_right[0:1] * root[0:1]
             own = {m: spread_row(column[0, m], j) for m in range(j + 1, STRIP)}
             ahead = {m: spread_row(column[1, j], m) for m in ready}
-            for group in groups:
+            for group in groups[0:2]:
                 weight = column[group, j] * inverse
                 if group == 0:
                     weight = jnp.where(iota == j, 1.0 - inverse, weight)
@@ -216,6 +216,11 @@
                         ready[m] = ready[m] - weight * ahead[m]
                 left[strip + group] = left[strip + group] - weight * row_left
                 right[strip + group] = right[strip + group] - weight * row_right
+        for j in range(STRIP):
+            for group in groups[2:]:
+                weight = column[group, j]
+                left[strip + group] = left[strip + group] - weight * spread_row(left[strip], j)
+                right[strip + group] = right[strip + group] - weight * spread_row(right[strip], j)
         last = first + STRIP * (LOOK + 1)
         if last < size:
             if strip > 0:
@@ -431,20 +436,20 @@
     exchange = functools.partial(
         lax.all_to_all, axis_name="rows", split_axis=0, concat_axis=0, tiled=True
     )
-    def routed(turn, pivots):
-        send, pick, turns, kept = pl.pallas_call(
+    def routed(turn, pivots, points, prior):
+        send, pick, turns, *kept = pl.pallas_call(
             pack_kernel,
             out_shape=(
                 jax.ShapeDtypeStruct((devices, 1, F), F32),
                 jax.ShapeDtypeStruct((8, devices), F32),
                 jax.ShapeDtypeStruct((1,), jnp.int32),
                 jax.ShapeDtypeStruct((PANELS, PANEL), jnp.int32),
+                jax.ShapeDtypeStruct((rows, D), F32),
+                jax.ShapeDtypeStruct((rows, R0), F32),
             ),
             in_specs=[SMEM, HBM, HBM, HBM],
-            out_specs=(HBM, VMEM, SMEM, VMEM),
+            out_specs=(HBM, VMEM, SMEM, VMEM, VMEM, VMEM),
             scratch_shapes=[
-                pltpu.VMEM((rows, D), F32),
-                pltpu.VMEM((rows, R0), F32),
                 pltpu.VMEM((devices, 1, F), F32),
                 pltpu.SemaphoreType.DMA((3,)),
                 pltpu.SemaphoreType.DMA((2,)),
@@ -463,8 +468,11 @@
         )(pick, exchange(send))
         return owned, turns[0], kept
 
-    owned, turns, pivots = routed(
-        jnp.zeros((1,), jnp.int32), pltpu.with_memory_space_constraint(pivots, pltpu.HBM)
+    owned, turns, (pivots, points, prior) = routed(
+        jnp.zeros((1,), jnp.int32),
+        pltpu.with_memory_space_constraint(pivots, pltpu.HBM),
+        pltpu.with_memory_space_constraint(points, pltpu.HBM),
+        pltpu.with_memory_space_constraint(prior, pltpu.HBM),
     )
 
     scale = inv_scale.reshape(1, D)
@@ -491,7 +499,7 @@
 
     def again(state):
         turn, owned = state
-        return turn + 1, owned + routed(turn[None], pivots)[0]
+        return turn + 1, owned + routed(turn[None], pivots, points, prior)[0]
 
     owned = lax.while_loop(more, again, (jnp.int32(1), owned))[1]
     mine = exchange(jnp.broadcast_to(owned, (homes, *owned.shape[1:])), axis_index_groups=groups)

time: 63.1 us -> 63.1 us (level)
  no operation moved by 1% of the time
where the time goes in v7:
time: 63.1 us; the launch traced here: 62.8 us
  Pallas kernels  18.2 us (29%)
  blocking collectives  17.3 us (27%)
  starting transfers between devices  14 us (22%)
  waiting for transfers between devices  10.2 us (16%)
  between operations  1.53 us (2%)
  local copies, waits for them, and re-layouts  0.99 us (2%)
  loops' own time  0.69 us (1%)
    all_to_all x1, blocking collectives, local(): exchange(jnp.broadcast_to(owned, (homes, *owned.shape[1:])), axis_index_g...  17.3 us
    pallas_call x1, Pallas kernels, local(): pl.pallas_call(window_kernel, out_shape=(jax.ShapeDtypeStruct((rows, PIV)...  12.5 us
    all_to_all x1, starting transfers between devices, routed(): exchange(send)  11.5 us
    all_to_all x1, waiting for transfers between devices, routed(): exchange(send)  10.2 us
    pallas_call x1, Pallas kernels, routed(): pl.pallas_call(pack_kernel, out_shape=(jax.ShapeDtypeStruct((devices, 1,...  3.23 us
    ppermute x1, starting transfers between devices, local(): other = lax.ppermute(mine, 'rows', partner)  2.46 us
  transfers between devices with their start and end apart: 2, of which 1 were waited for; matrix products, arithmetic and copies ran while one was open for 0% of the time, Pallas kernels for 4%

profile of v7, /device:TPU:1, one launch (start us, length us, event | category | flops | bytes accessed | tf_op | source)
XLA Modules:
  0.0 62.8 jit_solution(14383594443759792630)
XLA Ops:
  0.6 3.2 %pack.2 = (f32[128,1,768]{2,1,0:T(1,128)}, f32[8,128]{1,0:T(8,128)S(1)}, s32[1]{0:T(128)}, s32[3,128]{1,0:T(4,128)S(1)}, f32[384,256]{1,0:T(8,128)S(1)}, /*index=5*/f32[384,512]{1,0:T(8,128)S(1)}) custom-call(s32[1]{0:T(128)} %constant.1.clone.1.turn_ref, s32[3,128]{1,0:T(4,128)} %pivots_hbm.1, f32[384,256]{1,0:T(8,128)} %points_hbm.1, f32[384,512]{1,0:T(8,128)} %prior_hbm.1), custom_call_target="tpu_custom_call" | custom-call | tf_op jit(solution)/shard_map/pack/pallas_call | solution.py:440
  3.9 11.5 %all-to-all-start.1 = ((f32[128,1,768]{2,1,0:T(1,128)}), f32[128,1,768]{2,1,0:T(1,128)S(1)}, u32[]{:S(2)}, u32[]{:S(2)}) async-start(f32[128,1,768]{2,1,0:T(1,128)} %get-tuple-element.60), calls=%async_computation.1 | async-start | bytes 786432 | tf_op jit(solution)/shard_map/all_to_all | solution.py:468
  15.4 0.0 copy-start.1
  15.4 0.0 copy-start
  15.4 0.7 %copy-done.1 = s32[3,384]{1,0:T(4,128)S(1)} copy-done((s32[3,384]{1,0:T(4,128)S(1)}, s32[3,384]{1,0:T(4,128)}, u32[]{:S(2)}) %copy-start.1) | copy-done | bytes 4632
  16.1 0.0 copy-done
  16.1 1.2 %prepare.1 = (bf16[2,384,256]{2,1,0:T(8,128)(2,1)S(1)}, bf16[2,384,512]{2,1,0:T(8,128)(2,1)S(1)}, f32[2,384]{1,0:T(2,128)S(1)}, bf16[2,192,192]{2,1,0:T(8,128)(2,1)S(1)}, f32[3,384]{1,0:T(4,128)S(1)}) custom-call(s32[3,128]{1,0:T(4,128)S(1)} %get-tuple-element.137.pivots_ref, f32[1,256]{1,0:T(1,128)S(1)} %bitcast.5, ...), custom_call_target="tpu_custom_call" | custom-call | tf_op jit(solution)/shard_map/prepare/pallas_call | solution.py:479
  17.3 10.2 %all-to-all-done.1.came_ref = f32[128,1,768]{2,1,0:T(1,128)S(1)} async-done(((f32[128,1,768]{2,1,0:T(1,128)}), f32[128,1,768]{2,1,0:T(1,128)S(1)}, u32[]{:S(2)}, u32[]{:S(2)}) %all-to-all-start.1) | async-done | bytes 393248 | tf_op jit(solution)/shard_map/all_to_all | solution.py:468
  27.5 0.3 pick.2
  27.8 0.7 %while.10 = (s32[]{:T(128)}, f32[1,1,2304]{2,1,0:T(1,128)S(1)}, s32[]{:T(128)}, s32[3,128]{1,0:T(4,128)S(1)}, f32[384,256]{1,0:T(8,128)S(1)}, /*index=5*/f32[384,512]{1,0:T(8,128)S(1)}, s32[]{:T(128)}) while((s32[]{:T(128)}, f32[1,1,2304]{2,1,0:T(1,128)S(1)}, s32[]{:T(128)}, s32[3,128]{1,0:T(4,128)S(1)}, f32[384,256]{1,0:T(8,128)S(1)}, ...), condition=%wide.region_1.0_spmd, body=%wide.region_0.0_spmd.sunk | while | flops 2306 | bytes 1207405 | solution.py:504
  28.5 0.3 broadcast_in_dim.11
  28.8 17.3 %all_to_all.16.buf_ref = f32[64,1,2304]{2,1,0:T(1,128)S(1)} all-to-all(f32[64,1,2304]{2,1,0:T(1,128)S(1)} %broadcast_in_dim.11), channel_id=1, replica_groups={{0,2,4,6,8,10,12,14,16,18,20,22,24,26,28,30,32,34,36,38,40,42,44,46,48,..., dimensions={0} | all-to-all | bytes 1179648 | tf_op jit(solution)/shard_map/all_to_all | solution.py:505
  46.1 2.5 %collective-permute-start = (f32[64,1,2304]{2,1,0:T(1,128)S(1)}, f32[64,1,2304]{2,1,0:T(1,128)S(1)}, u32[]{:S(2)}, u32[]{:S(2)}) collective-permute-start(f32[64,1,2304]{2,1,0:T(1,128)S(1)} %all_to_all.16.buf_ref), channel_id=1, source_target_pairs={{0,1},{1,0},{2,3},{3,2},{4,5},{5,4},{6,7},{7,6},{8,9},{9,8},{10,11... | collective-permute-start | bytes 1769480 | tf_op jit(solution)/shard_map/ppermute | solution.py:506
  49.2 1.0 %half.1 = (bf16[2,192,256]{2,1,0:T(8,128)(2,1)S(1)}, bf16[2,192,512]{2,1,0:T(8,128)(2,1)S(1)}, f32[192,1]{1,0:T(8,128)S(1)}, f32[192,384]{1,0:T(8,128)S(1)}) custom-call(f32[1]{0:T(128)S(6)} %copy.14.noise_ref, s32[3,128]{1,0:T(4,128)S(1)} %get-tuple-element.159, f32[1,256]{1,0:T(1,128)S(1)} %bitcast.6, ...), custom_call_target="tpu_custom_call" | custom-call | tf_op jit(solution)/shard_map/half/pallas_call | solution.py:508
  50.2 0.0 collective-permute-done.buf_ref
  50.2 12.5 %window.1 = (f32[384,384]{1,0:T(8,128)}, f32[384]{0:T(512)}) custom-call(f32[1]{0:T(128)S(6)} %copy.14.noise_ref, s32[3,128]{1,0:T(4,128)S(1)} %get-tuple-element.159, f32[1,256]{1,0:T(1,128)S(1)} %bitcast.7, bf16[2,192,192]{2,1,0:T(8,128)(2,1)S(1)} %get-tuple-element.68.place_ref, f32[2,384]{1,0:T(2,128)S(1)} %get-tuple-element.69.sums_ref, ...), custom_call_target="tpu_custom_call" | custom-call | tf_op jit(solution)/shard_map/window/pallas_call | solution.py:522
  (1 shorter events, 0.0 us)
Async XLA Ops:
  3.9 23.6 %all-to-all-start.1 = ((f32[128,1,768]{2,1,0:T(1,128)}), f32[128,1,768]{2,1,0:T(1,128)S(1)}, u32[]{:S(2)}, u32[]{:S(2)}) async-start(f32[128,1,768]{2,1,0:T(1,128)} %get-tuple-element.60), calls=%async_computation.1 | async-start | bytes 786432 | tf_op jit(solution)/shard_map/all_to_all | solution.py:468
  15.4 0.7 %copy-start.1 = (s32[3,384]{1,0:T(4,128)S(1)}, s32[3,384]{1,0:T(4,128)}, u32[]{:S(2)}) copy-start(s32[3,384]{1,0:T(4,128)} %active_ref.1) | copy-start | bytes 13828
  15.4 0.7 %copy-start = (f32[256]{0:T(256)S(1)}, f32[256]{0:T(256)}, u32[]{:S(2)}) copy-start(f32[256]{0:T(256)} %param.9) | copy-start | bytes 3076
  46.1 4.1 %collective-permute-start = (f32[64,1,2304]{2,1,0:T(1,128)S(1)}, f32[64,1,2304]{2,1,0:T(1,128)S(1)}, u32[]{:S(2)}, u32[]{:S(2)}) collective-permute-start(f32[64,1,2304]{2,1,0:T(1,128)S(1)} %all_to_all.16.buf_ref), channel_id=1, source_target_pairs={{0,1},{1,0},{2,3},{3,2},{4,5},{5,4},{6,7},{7,6},{8,9},{9,8},{10,11... | collective-permute-start | bytes 1769480 | tf_op jit(solution)/shard_map/ppermute | solution.py:506

commit v8 on v7

--- a/solution.py
+++ b/solution.py
@@ -123,19 +123,9 @@
         step = place - place[:, 0:1] - homes * turn
         home = 2.0 * (place - homes * jnp.floor(place * (1.0 / homes))) + half
         home = jnp.where((found > 0.5) & (step >= 0.0) & (step < homes), home, -1.0)
-        start = count_halves([column < edges for column in columns])
-        stop = count_halves([column < edges + rows for column in columns])
-        step = wanted - start - homes * turn
-        mine = (wanted >= start) & (wanted < stop) & (step >= 0.0) & (step < homes)
-        mine = mine & (slot < HALF // homes) & (core == half)
         hit = target == home
-        run = jnp.max(stop - start)
         select = hit if half == 0 else select | hit
-        pick = mine if half == 0 else pick | mine
-        longest = run if half == 0 else jnp.maximum(longest, run)
     select = select.astype(BF)
-    pick_ref[...] = pick.astype(F32)
-    turns_ref[0] = jnp.where(longest > 2 * homes, 3, jnp.where(longest > homes, 2, 1))
     at = 0
     stores = []
     for load, ref in ((loads[1], points_ref), (loads[2], prior_ref)):
@@ -151,6 +141,17 @@
             )
         )
         stores[-1].start()
+    for half, columns in enumerate(halves(pivot_columns(pivots_ref))):
+        start = count_halves([column < edges for column in columns])
+        stop = count_halves([column < edges + rows for column in columns])
+        step = wanted - start - homes * turn
+        mine = (wanted >= start) & (wanted < stop) & (step >= 0.0) & (step < homes)
+        mine = mine & (slot < HALF // homes) & (core == half)
+        run = jnp.max(stop - start)
+        pick = mine if half == 0 else pick | mine
+        longest = run if half == 0 else jnp.maximum(longest, run)
+    pick_ref[...] = pick.astype(F32)
+    turns_ref[0] = jnp.where(longest > 2 * homes, 3, jnp.where(longest > homes, 2, 1))
     for store in stores:
         store.wait()
 

time: 63.1 us -> 63.2 us (level)
  no operation moved by 1% of the time
where the time goes in v8:
time: 63.2 us; the launch traced here: 62.9 us
  Pallas kernels  18.3 us (29%)
  blocking collectives  17.3 us (27%)
  starting transfers between devices  14 us (22%)
  waiting for transfers between devices  10.2 us (16%)
  between operations  1.53 us (2%)
  local copies, waits for them, and re-layouts  0.99 us (2%)
  loops' own time  0.69 us (1%)
    all_to_all x1, blocking collectives, local(): exchange(jnp.broadcast_to(owned, (homes, *owned.shape[1:])), axis_index_g...  17.3 us
    pallas_call x1, Pallas kernels, local(): pl.pallas_call(window_kernel, out_shape=(jax.ShapeDtypeStruct((rows, PIV)...  12.5 us
    all_to_all x1, starting transfers between devices, routed(): exchange(send)  11.5 us
    all_to_all x1, waiting for transfers between devices, routed(): exchange(send)  10.2 us
    pallas_call x1, Pallas kernels, routed(): pl.pallas_call(pack_kernel, out_shape=(jax.ShapeDtypeStruct((devices, 1,...  3.28 us
    ppermute x1, starting transfers between devices, local(): other = lax.ppermute(mine, 'rows', partner)  2.46 us
  transfers between devices with their start and end apart: 2, of which 1 were waited for; matrix products, arithmetic and copies ran while one was open for 0% of the time, Pallas kernels for 4%

profile of v8, /device:TPU:1, one launch (start us, length us, event | category | flops | bytes accessed | tf_op | source)
XLA Modules:
  0.0 62.9 jit_solution(1865972899297342930)
XLA Ops:
  0.6 3.3 %pack.2 = (f32[128,1,768]{2,1,0:T(1,128)}, f32[8,128]{1,0:T(8,128)S(1)}, s32[1]{0:T(128)}, s32[3,128]{1,0:T(4,128)S(1)}, f32[384,256]{1,0:T(8,128)S(1)}, /*index=5*/f32[384,512]{1,0:T(8,128)S(1)}) custom-call(s32[1]{0:T(128)} %constant.1.clone.1.turn_ref, s32[3,128]{1,0:T(4,128)} %pivots_hbm.1, f32[384,256]{1,0:T(8,128)} %points_hbm.1, f32[384,512]{1,0:T(8,128)} %prior_hbm.1), custom_call_target="tpu_custom_call" | custom-call | tf_op jit(solution)/shard_map/pack/pallas_call | solution.py:441
  3.9 11.5 %all-to-all-start.1 = ((f32[128,1,768]{2,1,0:T(1,128)}), f32[128,1,768]{2,1,0:T(1,128)S(1)}, u32[]{:S(2)}, u32[]{:S(2)}) async-start(f32[128,1,768]{2,1,0:T(1,128)} %get-tuple-element.60), calls=%async_computation.1 | async-start | bytes 786432 | tf_op jit(solution)/shard_map/all_to_all | solution.py:469
  15.4 0.0 copy-start.1
  15.4 0.0 copy-start
  15.4 0.7 %copy-done.1 = s32[3,384]{1,0:T(4,128)S(1)} copy-done((s32[3,384]{1,0:T(4,128)S(1)}, s32[3,384]{1,0:T(4,128)}, u32[]{:S(2)}) %copy-start.1) | copy-done | bytes 4632
  16.1 0.0 copy-done
  16.1 1.2 %prepare.1 = (bf16[2,384,256]{2,1,0:T(8,128)(2,1)S(1)}, bf16[2,384,512]{2,1,0:T(8,128)(2,1)S(1)}, f32[2,384]{1,0:T(2,128)S(1)}, bf16[2,192,192]{2,1,0:T(8,128)(2,1)S(1)}, f32[3,384]{1,0:T(4,128)S(1)}) custom-call(s32[3,128]{1,0:T(4,128)S(1)} %get-tuple-element.137.pivots_ref, f32[1,256]{1,0:T(1,128)S(1)} %bitcast.5, ...), custom_call_target="tpu_custom_call" | custom-call | tf_op jit(solution)/shard_map/prepare/pallas_call | solution.py:480
  17.4 10.2 %all-to-all-done.1.came_ref = f32[128,1,768]{2,1,0:T(1,128)S(1)} async-done(((f32[128,1,768]{2,1,0:T(1,128)}), f32[128,1,768]{2,1,0:T(1,128)S(1)}, u32[]{:S(2)}, u32[]{:S(2)}) %all-to-all-start.1) | async-done | bytes 393248 | tf_op jit(solution)/shard_map/all_to_all | solution.py:469
  27.6 0.3 pick.2
  27.8 0.7 %while.10 = (s32[]{:T(128)}, f32[1,1,2304]{2,1,0:T(1,128)S(1)}, s32[]{:T(128)}, s32[3,128]{1,0:T(4,128)S(1)}, f32[384,256]{1,0:T(8,128)S(1)}, /*index=5*/f32[384,512]{1,0:T(8,128)S(1)}, s32[]{:T(128)}) while((s32[]{:T(128)}, f32[1,1,2304]{2,1,0:T(1,128)S(1)}, s32[]{:T(128)}, s32[3,128]{1,0:T(4,128)S(1)}, f32[384,256]{1,0:T(8,128)S(1)}, ...), condition=%wide.region_1.0_spmd, body=%wide.region_0.0_spmd.sunk | while | flops 2306 | bytes 1207405 | solution.py:505
  28.6 0.3 broadcast_in_dim.11
  28.9 17.3 %all_to_all.16.buf_ref = f32[64,1,2304]{2,1,0:T(1,128)S(1)} all-to-all(f32[64,1,2304]{2,1,0:T(1,128)S(1)} %broadcast_in_dim.11), channel_id=1, replica_groups={{0,2,4,6,8,10,12,14,16,18,20,22,24,26,28,30,32,34,36,38,40,42,44,46,48,..., dimensions={0} | all-to-all | bytes 1179648 | tf_op jit(solution)/shard_map/all_to_all | solution.py:506
  46.2 2.5 %collective-permute-start = (f32[64,1,2304]{2,1,0:T(1,128)S(1)}, f32[64,1,2304]{2,1,0:T(1,128)S(1)}, u32[]{:S(2)}, u32[]{:S(2)}) collective-permute-start(f32[64,1,2304]{2,1,0:T(1,128)S(1)} %all_to_all.16.buf_ref), channel_id=1, source_target_pairs={{0,1},{1,0},{2,3},{3,2},{4,5},{5,4},{6,7},{7,6},{8,9},{9,8},{10,11... | collective-permute-start | bytes 1769480 | tf_op jit(solution)/shard_map/ppermute | solution.py:507
  49.3 1.0 %half.1 = (bf16[2,192,256]{2,1,0:T(8,128)(2,1)S(1)}, bf16[2,192,512]{2,1,0:T(8,128)(2,1)S(1)}, f32[192,1]{1,0:T(8,128)S(1)}, f32[192,384]{1,0:T(8,128)S(1)}) custom-call(f32[1]{0:T(128)S(6)} %copy.14.noise_ref, s32[3,128]{1,0:T(4,128)S(1)} %get-tuple-element.159, f32[1,256]{1,0:T(1,128)S(1)} %bitcast.6, ...), custom_call_target="tpu_custom_call" | custom-call | tf_op jit(solution)/shard_map/half/pallas_call | solution.py:509
  50.3 0.0 collective-permute-done.buf_ref
  50.3 12.5 %window.1 = (f32[384,384]{1,0:T(8,128)}, f32[384]{0:T(512)}) custom-call(f32[1]{0:T(128)S(6)} %copy.14.noise_ref, s32[3,128]{1,0:T(4,128)S(1)} %get-tuple-element.159, f32[1,256]{1,0:T(1,128)S(1)} %bitcast.7, bf16[2,192,192]{2,1,0:T(8,128)(2,1)S(1)} %get-tuple-element.68.place_ref, f32[2,384]{1,0:T(2,128)S(1)} %get-tuple-element.69.sums_ref, ...), custom_call_target="tpu_custom_call" | custom-call | tf_op jit(solution)/shard_map/window/pallas_call | solution.py:523
  (1 shorter events, 0.0 us)
Async XLA Ops:
  3.9 23.6 %all-to-all-start.1 = ((f32[128,1,768]{2,1,0:T(1,128)}), f32[128,1,768]{2,1,0:T(1,128)S(1)}, u32[]{:S(2)}, u32[]{:S(2)}) async-start(f32[128,1,768]{2,1,0:T(1,128)} %get-tuple-element.60), calls=%async_computation.1 | async-start | bytes 786432 | tf_op jit(solution)/shard_map/all_to_all | solution.py:469
  15.4 0.7 %copy-start.1 = (s32[3,384]{1,0:T(4,128)S(1)}, s32[3,384]{1,0:T(4,128)}, u32[]{:S(2)}) copy-start(s32[3,384]{1,0:T(4,128)} %active_ref.1) | copy-start | bytes 13828
  15.4 0.7 %copy-start = (f32[256]{0:T(256)S(1)}, f32[256]{0:T(256)}, u32[]{:S(2)}) copy-start(f32[256]{0:T(256)} %param.9) | copy-start | bytes 3076
  46.2 4.1 %collective-permute-start = (f32[64,1,2304]{2,1,0:T(1,128)S(1)}, f32[64,1,2304]{2,1,0:T(1,128)S(1)}, u32[]{:S(2)}, u32[]{:S(2)}) collective-permute-start(f32[64,1,2304]{2,1,0:T(1,128)S(1)} %all_to_all.16.buf_ref), channel_id=1, source_target_pairs={{0,1},{1,0},{2,3},{3,2},{4,5},{5,4},{6,7},{7,6},{8,9},{9,8},{10,11... | collective-permute-start | bytes 1769480 | tf_op jit(solution)/shard_map/ppermute | solution.py:507
